TPU v7x, 512 devices: a whole 4x8x8 slice. The times are simulated.
512 devices in a mesh: tile: 16 (over z, core), img: 32 (over x, y).
Axes of the slice: x: 4, y: 8, z: 8, core: 2. Of those that a mesh axis runs over, the one named last changes fastest.
Arguments:
- qkv: bfloat16 [32, 16, 8, 32, 1536], P('img', 'tile'), may hold values from -6 to 6
- cotangent: bfloat16 [32, 16, 8, 32, 1024], P('img', 'tile'), may hold values from -48 to 48
- dw_weight: float32 [25, 1536], replicated, may hold values from -1.25 to 1.25
- pw_weight: float32 [32, 1536], replicated, may hold values from -1 to 1
- tile_image: int32 [32, 16], P('img', 'tile'), may hold values from 0 to 8, as said below
- tile_row: int32 [32, 16], P('img', 'tile'), may hold values from 0 to 7, as said below
- tile_col: int32 [32, 16], P('img', 'tile'), may hold values from 0 to 1, as said below
- image_height: int32 [32, 8], P('img'), may hold values from 0 to 8, as said below
- image_width: int32 [32, 8], P('img'), may hold values from 0 to 2, as said below
Outputs:
- grad_qkv: bfloat16 [32, 16, 8, 32, 1536], P('img', 'tile')
- grad_dw: float32 [25, 1536], replicated
- grad_pw: float32 [32, 1536], replicated
Inputs may be any that keep to these rules, and one draw needn't show every extreme that they name: Within a group tile_image never falls; each image occupies height * width consecutive tiles; padding tiles come last; the first group holds 8 images of 1 x 2 tiles; the second group holds one image of 8 x 2 tiles. `tile_row`: the tile's row in its image's grid, row-major order; 0 on padding tiles. `tile_col`: the tile's column in its image's grid; 0 on padding tiles. `image_height`: used slots come first; an unused slot has height 0. `image_width`: used slots come first; an unused slot has width 0.
All inputs are finite; a program needn't handle non-finite values.
Results may differ from a plain program's by a relative error of at most 0.005.
Values may be sent and summed in bfloat16 or wider, within the bound.
A program may use at most 64 MiB of HBM per device.

v0:
```python
import math

import jax
import jax.numpy as jnp
from jax import lax
from jax.sharding import PartitionSpec as P

PRECISE = lax.Precision.HIGHEST
EPSILON = 1e-06


def from_behind(value, axis, steps):
    count = lax.axis_size(axis)
    initial, last = (max(0, -steps), min(count, count - steps))
    return lax.ppermute(value, axis, [(source, source + steps) for source in range(initial, last)])


def shortened(x):

    def short(part):
        return part.astype(jnp.bfloat16) if part.dtype == jnp.float32 else part

    return jax.tree.map(short, x)


def widen_source(field, neighbours, image_wide):
    has_left, has_right, has_above, has_below = neighbours
    nothing = jnp.zeros((), field.dtype)
    side_cols = []
    for offset, outgoing in ((1, field[:, -2:]), (-1, field[:, :2])):
        side_cols.append(from_behind(outgoing, "tile", offset))
    widened = jnp.concatenate(
        [
            jnp.where(has_left, side_cols[0], nothing),
            field,
            jnp.where(has_right, side_cols[1], nothing),
        ],
        axis=1,
    )
    edge_rows = []
    for offset, outgoing in (
        (1, widened[-2:]),
        (2, widened[-2:]),
        (-1, widened[:2]),
        (-2, widened[:2]),
    ):
        edge_rows.append(from_behind(outgoing, "tile", offset))
    above_rows = jnp.where(image_wide == 1, edge_rows[0], edge_rows[1])
    below_rows = jnp.where(image_wide == 1, edge_rows[2], edge_rows[3])
    return jnp.concatenate(
        [
            jnp.where(has_above, above_rows, nothing),
            widened,
            jnp.where(has_below, below_rows, nothing),
        ],
        axis=0,
    )


def widen_grad(field, neighbours, image_wide):
    has_left, has_right, has_above, has_below = neighbours
    nothing = jnp.zeros((), field.dtype)
    side_cols = []
    for offset, outgoing in ((1, field[:, -2:]), (-1, field[:, :2])):
        side_cols.append(from_behind(shortened(outgoing), "tile", offset).astype(outgoing.dtype))
    widened = jnp.concatenate(
        [
            jnp.where(has_left, side_cols[0], nothing),
            field,
            jnp.where(has_right, side_cols[1], nothing),
        ],
        axis=1,
    )
    edge_rows = []
    for offset, outgoing in (
        (1, widened[-2:]),
        (2, widened[-2:]),
        (-1, widened[:2]),
        (-2, widened[:2]),
    ):
        edge_rows.append(from_behind(shortened(outgoing), "tile", offset).astype(outgoing.dtype))
    above_rows = jnp.where(image_wide == 1, edge_rows[0], edge_rows[1])
    below_rows = jnp.where(image_wide == 1, edge_rows[2], edge_rows[3])
    return jnp.concatenate(
        [
            jnp.where(has_above, above_rows, nothing),
            widened,
            jnp.where(has_below, below_rows, nothing),
        ],
        axis=0,
    )


def depthwise(padded, kernel, flipped):
    channels = padded.shape[2]
    shaped = kernel.reshape(5, 5, 1, channels)
    if flipped:
        shaped = shaped[::-1, ::-1]
    result = lax.conv_general_dilated(
        padded[None],
        shaped,
        (1, 1),
        "VALID",
        dimension_numbers=("NHWC", "HWIO", "NHWC"),
        feature_group_count=channels,
        precision=PRECISE,
    )
    return result[0]


def kernel_grad(padded, kernel, grad_mixed):

    def local_conv(weights):
        return depthwise(padded, weights, False)

    pullback = jax.vjp(local_conv, kernel)[1]
    return pullback(grad_mixed)[0]


def block_weights(pw_weight):
    head_dim, channels = pw_weight.shape
    per_block = 128 // head_dim
    nblocks = channels // 128
    pieces = pw_weight.reshape(head_dim, nblocks, per_block, head_dim).transpose(1, 0, 2, 3)
    identity = jnp.eye(per_block, dtype=jnp.float32)
    blocked = pieces[:, None, :, :, :] * identity[None, :, None, :, None]
    return blocked.reshape(nblocks, 128, 128)


def pointwise(flat, blocks, backward):
    positions, channels = flat.shape
    shaped = flat.reshape(positions, channels // 128, 128)
    if backward:
        result = jnp.einsum("pbo,bio->pbi", shaped, blocks, precision=PRECISE)
    else:
        result = jnp.einsum("pbi,bio->pbo", shaped, blocks, precision=PRECISE)
    return result.reshape(positions, channels)


def block_grad(flat_mixed, grad_merged, head_dim):
    positions, channels = flat_mixed.shape
    nblocks = channels // 128
    per_block = 128 // head_dim
    blocked = jnp.einsum(
        "pbi,pbo->bio",
        flat_mixed.reshape(positions, nblocks, 128),
        grad_merged.reshape(positions, nblocks, 128),
        precision=PRECISE,
    )
    blocked = blocked.reshape(nblocks, per_block, head_dim, per_block, head_dim)
    diagonal = jnp.einsum(
        "bgiho,gh->ibho", blocked, jnp.eye(per_block, dtype=jnp.float32), precision=PRECISE
    )
    return diagonal.reshape(head_dim, channels)


def head_parts(flat, head_count):
    positions = flat.shape[0]
    third = flat.shape[1] // 3
    return [
        flat[:, member * third : (member + 1) * third].reshape(
            positions, head_count, third // head_count
        )
        for member in range(3)
    ]


def image_total(states, key_sums, image_slot, slot_count):
    picker = (jnp.arange(slot_count) == image_slot).astype(jnp.float32)
    spread_states = picker[:, None, None, None] * states[None]
    spread_sums = picker[:, None, None] * key_sums[None]
    summed_states, summed_sums = lax.psum((spread_states, spread_sums), "tile")
    return (
        jnp.sum(picker[:, None, None, None] * summed_states, axis=0),
        jnp.sum(picker[:, None, None] * summed_sums, axis=0),
    )


def local(
    qkv, cotangent, dw_weight, pw_weight, tile_image, tile_row, tile_col, image_height, image_width
):
    tile_tall, tile_broad, channels = (qkv.shape[2], qkv.shape[3], qkv.shape[4])
    positions = tile_tall * tile_broad
    slot_count = image_height.shape[1]
    head_dim = pw_weight.shape[0]
    head_count = channels // (3 * head_dim)
    inner_width = head_count * head_dim
    image_slot = tile_image[0, 0]
    picker = jnp.arange(slot_count) == image_slot
    image_tall = jnp.sum(jnp.where(picker, image_height[0], 0))
    image_wide = jnp.sum(jnp.where(picker, image_width[0], 0))
    is_live = image_slot < slot_count
    grid_row = tile_row[0, 0]
    grid_col = tile_col[0, 0]
    neighbours = (
        is_live & (grid_col > 0),
        is_live & (grid_col < image_wide - 1),
        is_live & (grid_row > 0),
        is_live & (grid_row < image_tall - 1),
    )
    source = jnp.where(is_live, qkv[0, 0], jnp.zeros((), jnp.bfloat16))
    padded = widen_source(source, neighbours, image_wide).astype(jnp.float32)
    mixed_dw = depthwise(padded, dw_weight, False)
    flat_mixed = mixed_dw.reshape(positions, channels)
    blocks = block_weights(pw_weight)
    merged = pointwise(flat_mixed, blocks, False)
    central = padded[2 : 2 + tile_tall, 2 : 2 + tile_broad].reshape(positions, channels)
    scale_parts = []
    local_states = []
    local_sums = []
    for scale_input in (central, merged):
        raw_queries, raw_keys, values = head_parts(scale_input, head_count)
        queries = jax.nn.relu(raw_queries)
        key_rows = jax.nn.relu(raw_keys)
        scale_parts.append((raw_queries, raw_keys, queries, key_rows, values))
        local_states.append(
            jnp.einsum("phi,phj->ihj", key_rows, values, precision=PRECISE).reshape(
                head_dim, inner_width
            )
        )
        local_sums.append(jnp.sum(key_rows, axis=0).reshape(inner_width))
    states, key_sums = image_total(
        jnp.stack(local_states), jnp.stack(local_sums), image_slot, slot_count
    )
    cot_flat = cotangent[0, 0].astype(jnp.float32).reshape(positions, 2 * inner_width)
    grad_num_all = []
    local_gstates = []
    local_gsums = []
    for member in range(2):
        raw_queries, raw_keys, queries, key_rows, values = scale_parts[member]
        scale_state = states[member].reshape(head_dim, head_count, head_dim)
        scale_sum = key_sums[member].reshape(head_count, head_dim)
        numerator = jnp.einsum("phi,ihj->phj", queries, scale_state, precision=PRECISE)
        denominator = jnp.einsum("phi,hi->ph", queries, scale_sum, precision=PRECISE) + EPSILON
        result = numerator / denominator[..., None]
        grad_out = cot_flat[:, member * inner_width : (member + 1) * inner_width].reshape(
            positions, head_count, head_dim
        )
        grad_num = grad_out / denominator[..., None]
        grad_den = -jnp.sum(grad_out * result, axis=-1) / denominator
        grad_query = (
            jnp.einsum("phj,ihj->phi", grad_num, scale_state, precision=PRECISE)
            + grad_den[..., None] * scale_sum[None]
        )
        grad_num_all.append(grad_query)
        local_gstates.append(
            jnp.einsum("phi,phj->ihj", queries, grad_num, precision=PRECISE).reshape(
                head_dim, inner_width
            )
        )
        local_gsums.append(
            jnp.einsum("phi,ph->hi", queries, grad_den, precision=PRECISE).reshape(inner_width)
        )
    grad_states, grad_sums = image_total(
        jnp.stack(local_gstates), jnp.stack(local_gsums), image_slot, slot_count
    )
    scale_grads = []
    for member in range(2):
        raw_queries, raw_keys, queries, key_rows, values = scale_parts[member]
        gstate = grad_states[member].reshape(head_dim, head_count, head_dim)
        gsum = grad_sums[member].reshape(head_count, head_dim)
        grad_keys = jnp.einsum("phj,ihj->phi", values, gstate, precision=PRECISE) + gsum[None]
        grad_values = jnp.einsum("phi,ihj->phj", key_rows, gstate, precision=PRECISE)
        grad_queries = jnp.where(raw_queries > 0, grad_num_all[member], 0.0)
        grad_keys = jnp.where(raw_keys > 0, grad_keys, 0.0)
        scale_grads.append(
            jnp.concatenate(
                [
                    grad_queries.reshape(positions, inner_width),
                    grad_keys.reshape(positions, inner_width),
                    grad_values.reshape(positions, inner_width),
                ],
                axis=1,
            )
        )
    grad_merged = scale_grads[1]
    grad_mixed = pointwise(grad_merged, blocks, True)
    grad_pwk = block_grad(flat_mixed, grad_merged, head_dim)
    grad_field = grad_mixed.reshape(tile_tall, tile_broad, channels)
    grad_dwk = kernel_grad(padded, dw_weight, grad_field)
    grad_padded = widen_grad(grad_field, neighbours, image_wide)
    grad_through = depthwise(grad_padded, dw_weight, True)
    grad_source = scale_grads[0].reshape(tile_tall, tile_broad, channels) + grad_through
    grad_source = jnp.where(is_live, grad_source, 0.0).astype(jnp.bfloat16)
    summed_dw, summed_pw = lax.psum((grad_dwk, grad_pwk), ("tile", "img"))
    weight_norm = 1.0 / math.sqrt(positions * lax.axis_size("tile") * lax.axis_size("img"))
    return (grad_source[None, None], summed_dw * weight_norm, summed_pw * weight_norm)


def solution(mesh):
    placed = (
        P("img", "tile", None, None, None),
        P("img", "tile", None, None, None),
        P(),
        P(),
        P("img", "tile"),
        P("img", "tile"),
        P("img", "tile"),
        P("img", None),
        P("img", None),
    )
    return jax.shard_map(
        local,
        mesh=mesh,
        in_specs=placed,
        out_specs=(P("img", "tile", None, None, None), P(), P()),
        check_vma=False,
    )
```

profile of v0, /device:TPU:1, one launch (start us, length us, event | category | flops | bytes accessed | tf_op | source)
XLA Modules:
  0.0 720.6 jit_solution(15396547145481323407)
XLA Ops:
  10.0 5.4 collective-permute-start
  15.4 4.7 collective-permute-start.1
  31.2 3.2 collective-permute-start.2
  40.1 2.2 mul.67
  46.9 3.9 collective-permute-done.4
  50.8 4.3 collective-permute-done.5
  55.1 2.3 fusion.70
  59.8 3.6 convolution_select_fusion
  69.0 2.8 fusion.43
  73.5 44.7 %psum.43 = f32[8,2,512]{2,0,1:T(8,128)S(1)} all-reduce(f32[8,2,512]{2,0,1:T(8,128)S(1)} %broadcast_multiply_fusion.5), channel_id=1, replica_groups=mesh['tile'=16,'img'=32] {'tile'}, use_global_device_ids=true, to_apply=%region_6.7 | all-reduce | flops 8192 | bytes 65536 | tf_op jit(solution)/shard_map/psum | solution.py:172
  122.4 2.5 fusion.48
  126.0 2.6 fusion.49
  138.4 2.3 broadcast_multiply_fusion
  145.7 122.8 %all-reduce.7.cloned.1.call-done = (f32[8,2,32,512]{3,2,1,0:T(8,128)}, f32[8,2,32,512]{3,2,1,0:T(8,128)}) async-done(((f32[8,2,32,512]{3,2,1,0:T(8,128)}, f32[8,2,32,512]{3,2,1,0:T(8,128)}), (f32[8,2,32,512]{3,2,1,0:T(8,128)}, f32[8,2,32,512]{3,2,1,0:T(8,128)})) %all-reduce.7.cloned.1.call-update) | async-done | bytes 2097168 | tf_op jit(solution)/shard_map/psum | solution.py:172
  282.6 2.6 fusion.33
  287.8 45.7 %psum.45 = f32[8,2,512]{2,0,1:T(8,128)S(1)} all-reduce(f32[8,2,512]{2,0,1:T(8,128)S(1)} %broadcast_multiply_fusion.4), channel_id=1, replica_groups=mesh['tile'=16,'img'=32] {'tile'}, use_global_device_ids=true, to_apply=%region_12.13 | all-reduce | flops 8192 | bytes 65536 | tf_op jit(solution)/shard_map/psum | solution.py:172
  333.7 2.5 fusion.35
  337.5 2.6 fusion.41
  345.1 3.9 broadcast_in_dim_reshape_reshape.4
  351.3 33.5 %fusion.38 = f32[5,5,1536]{2,1,0:T(8,128)S(1)} fusion(f32[1,8,32,1536]{3,0,2,1:T(1,128)} %broadcast_in_dim_reshape_reshape.4, bf16[1,12,36,1536]{3,2,1,0:T(8,128)(2,1)} %get-tuple-element.26), kind=kOutput, calls=%fused_computation.50 | convolution fusion | flops 117964800 | bytes 3053568 | tf_op jit(solution)/shard_map/transpose(jvp())/conv_general_dilated | solution.py:99
  386.3 3.6 collective-permute-start.6
  389.9 4.0 collective-permute-start.7
  393.9 2.9 reshape.202
  396.9 2.2 fusion.27
  399.1 6.7 fusion.6
  408.1 3.0 copy.171
  413.0 3.0 copy.172
  417.8 3.0 copy.170
  425.8 2.5 collective-permute-start.8
  431.8 262.4 %all-reduce.5.cloned.1.call-done = (f32[25,1536]{1,0:T(8,128)}, f32[32,1536]{1,0:T(8,128)}) async-done(((f32[25,1536]{1,0:T(8,128)}, f32[32,1536]{1,0:T(8,128)}), (f32[25,1536]{1,0:T(8,128)}, f32[32,1536]{1,0:T(8,128)})) %all-reduce.5.cloned.1.call-update) | async-done | bytes 350224 | tf_op jit(solution)/shard_map/psum | solution.py:285
  698.2 4.7 reshape.213
  705.8 3.4 fusion.8
  (223 shorter events, 102.2 us)
Async XLA Ops:
  7.2 12.9 %copy-start.8 = (bf16[1,1,8,32,1536]{4,3,2,1,0:T(8,128)(2,1)S(1)}, bf16[1,1,8,32,1536]{4,3,2,1,0:T(8,128)(2,1)}, u32[]{:S(2)}) copy-start(bf16[1,1,8,32,1536]{4,3,2,1,0:T(8,128)(2,1)} %param.9) | copy-start | bytes 2359300
  7.2 12.9 %copy-start.17 = (bf16[1,1,8,32,1024]{4,3,2,1,0:T(8,128)(2,1)S(1)}, bf16[1,1,8,32,1024]{4,3,2,1,0:T(8,128)(2,1)}, u32[]{:S(2)}) copy-start(bf16[1,1,8,32,1024]{4,3,2,1,0:T(8,128)(2,1)} %param.10) | copy-start | bytes 1572868
  7.2 261.4 %all-reduce.7.cloned.1.call-start = ((), (), s32[]{:S(2)}) async-start(), calls=%async_computation.1 | async-start | bytes 4194304 | tf_op jit(solution)/shard_map/psum | solution.py:172
  9.2 19.1 %copy-start.1 = (bf16[8,32,1536]{2,1,0:T(8,128)(2,1)}, bf16[8,32,1536]{2,1,0:T(8,128)(2,1)S(1)}, u32[]{:S(2)}) copy-start(bf16[8,32,1536]{2,1,0:T(8,128)(2,1)S(1)} %fusion.115) | copy-start | bytes 2359300
  10.0 18.1 %collective-permute-start = (bf16[8,2,1536]{2,1,0:T(2,128)(2,1)S(1)}, bf16[8,2,1536]{2,1,0:T(2,128)(2,1)S(1)}, u32[]{:S(2)}, u32[]{:S(2)}) collective-permute-start(bf16[8,2,1536]{2,1,0:T(2,128)(2,1)S(1)} %get-tuple-element.34), channel_id=1, source_target_pairs={{0,32},{32,64},{64,96},{96,128},{128,160},{160,192},{192,224},{224... | collective-permute-start | bytes 147464 | tf_op jit(solution)/shard_map/ppermute | solution.py:15
  15.4 12.8 %collective-permute-start.1 = (bf16[8,2,1536]{2,1,0:T(2,128)(2,1)}, bf16[8,2,1536]{2,1,0:T(2,128)(2,1)S(1)}, u32[]{:S(2)}, u32[]{:S(2)}) collective-permute-start(bf16[8,2,1536]{2,1,0:T(2,128)(2,1)} %get-tuple-element.35), channel_id=1, source_target_pairs={{32,0},{64,32},{96,64},{128,96},{160,128},{192,160},{224,192},{256... | collective-permute-start | bytes 147464 | tf_op jit(solution)/shard_map/ppermute | solution.py:15
  22.9 107.4 %copy-start.10 = (bf16[256,512]{0,1:T(8,128)(2,1)}, bf16[256,512]{0,1:T(8,128)(2,1)S(1)}, u32[]{:S(2)}) copy-start(bf16[256,512]{0,1:T(8,128)(2,1)S(1)} %slice.113) | copy-start | bytes 786436
  22.9 11.8 %copy-start.24 = (f32[32,1536]{1,0:T(8,128)S(1)}, f32[32,1536]{1,0:T(8,128)}, u32[]{:S(2)}) copy-start(f32[32,1536]{1,0:T(8,128)} %param.12) | copy-start | bytes 589828
  28.2 7.9 %copy-start.16 = (f32[256,512]{1,0:T(8,128)S(1)}, f32[256,512]{1,0:T(8,128)}, u32[]{:S(2)}) copy-start(f32[256,512]{1,0:T(8,128)} %get-tuple-element.28) | copy-start | bytes 1572868
  29.2 16.7 %collective-permute-start.3 = (bf16[2,36,1536]{2,1,0:T(8,128)(2,1)}, bf16[2,36,1536]{2,1,0:T(8,128)(2,1)}, u32[]{:S(2)}, u32[]{:S(2)}) collective-permute-start(bf16[2,36,1536]{2,1,0:T(8,128)(2,1)} %get-tuple-element.30), channel_id=1, source_target_pairs={{0,64},{32,96},{64,128},{96,160},{128,192},{160,224},{192,256},{22... | collective-permute-start | bytes 663560 | tf_op jit(solution)/shard_map/ppermute | solution.py:15
  31.2 14.7 %collective-permute-start.2 = (bf16[2,36,1536]{2,1,0:T(8,128)(2,1)}, bf16[2,36,1536]{2,1,0:T(8,128)(2,1)}, u32[]{:S(2)}, u32[]{:S(2)}) collective-permute-start(bf16[2,36,1536]{2,1,0:T(8,128)(2,1)} %get-tuple-element.30), channel_id=1, source_target_pairs={{0,32},{32,64},{64,96},{96,128},{128,160},{160,192},{192,224},{224... | collective-permute-start | bytes 663560 | tf_op jit(solution)/shard_map/ppermute | solution.py:15
  42.3 12.8 %copy-start.2 = (bf16[8,32,1536]{2,1,0:T(8,128)(2,1)S(1)}, bf16[8,32,1536]{2,1,0:T(8,128)(2,1)}, u32[]{:S(2)}) copy-start(bf16[8,32,1536]{2,1,0:T(8,128)(2,1)} %copy-done.1) | copy-start | bytes 2359300
  42.3 75.8 %copy-start.34 = (f32[8]{0:T(128)}, f32[8]{0:T(128)S(1)}, u32[]{:S(2)}) copy-start(f32[8]{0:T(128)S(1)} %fusion.60) | copy-start | bytes 100
  42.3 8.5 %collective-permute-start.4 = (bf16[2,36,1536]{2,1,0:T(8,128)(2,1)}, bf16[2,36,1536]{2,1,0:T(8,128)(2,1)S(1)}, u32[]{:S(2)}, u32[]{:S(2)}) collective-permute-start(bf16[2,36,1536]{2,1,0:T(8,128)(2,1)} %get-tuple-element.31), channel_id=1, source_target_pairs={{32,0},{64,32},{96,64},{128,96},{160,128},{192,160},{224,192},{256... | collective-permute-start | bytes 663560 | tf_op jit(solution)/shard_map/ppermute | solution.py:15
  44.4 10.7 %collective-permute-start.5 = (bf16[2,36,1536]{2,1,0:T(8,128)(2,1)}, bf16[2,36,1536]{2,1,0:T(8,128)(2,1)S(1)}, u32[]{:S(2)}, u32[]{:S(2)}) collective-permute-start(bf16[2,36,1536]{2,1,0:T(8,128)(2,1)} %get-tuple-element.31), channel_id=1, source_target_pairs={{64,0},{96,32},{128,64},{160,96},{192,128},{224,160},{256,192},{28... | collective-permute-start | bytes 663560 | tf_op jit(solution)/shard_map/ppermute | solution.py:15
  140.7 127.8 %copy-start.35 = (f32[8]{0:T(128)S(1)}, f32[8]{0:T(128)}, u32[]{:S(2)}) copy-start(f32[8]{0:T(128)} %copy-done.34) | copy-start | bytes 100
  140.8 553.4 %all-reduce.5.cloned.1.call-start = ((), (), s32[]{:S(2)}) async-start(), calls=%async_computation | async-start | bytes 786432 | tf_op jit(solution)/shard_map/psum | solution.py:285
  145.7 125.5 %copy-start.7 = (f32[256,512]{0,1:T(8,128)S(1)}, f32[256,512]{0,1:T(8,128)}, u32[]{:S(2)}) copy-start(f32[256,512]{0,1:T(8,128)} %get-tuple-element.45) | copy-start | bytes 1572868
  272.7 8.2 %copy-start.5 = (f32[256,512]{0,1:T(8,128)S(1)}, f32[256,512]{0,1:T(8,128)}, u32[]{:S(2)}) copy-start(f32[256,512]{0,1:T(8,128)} %get-tuple-element.46) | copy-start | bytes 1572868
  384.7 9.2 %copy-start.9 = (f32[12,128,128]{2,1,0:T(8,128)S(1)}, f32[12,128,128]{2,1,0:T(8,128)}, u32[]{:S(2)}) copy-start(f32[12,128,128]{2,1,0:T(8,128)} %fusion.41) | copy-start | bytes 2359300
  386.3 36.4 %collective-permute-start.6 = (bf16[8,2,1536]{2,1,0:T(2,128)(2,1)}, bf16[8,2,1536]{2,1,0:T(2,128)(2,1)}, u32[]{:S(2)}, u32[]{:S(2)}) collective-permute-start(bf16[8,2,1536]{2,1,0:T(2,128)(2,1)} %get-tuple-element.32), channel_id=1, source_target_pairs={{0,32},{32,64},{64,96},{96,128},{128,160},{160,192},{192,224},{224... | collective-permute-start | bytes 147464 | tf_op jit(solution)/shard_map/ppermute | solution.py:15
  389.9 7.0 copy-start.20
  389.9 7.0 copy-start.22
  389.9 7.0 copy-start.29
  389.9 7.0 copy-start.31
  389.9 33.6 %collective-permute-start.7 = (bf16[8,2,1536]{2,1,0:T(2,128)(2,1)}, bf16[8,2,1536]{2,1,0:T(2,128)(2,1)}, u32[]{:S(2)}, u32[]{:S(2)}) collective-permute-start(bf16[8,2,1536]{2,1,0:T(2,128)(2,1)} %get-tuple-element.33), channel_id=1, source_target_pairs={{32,0},{64,32},{96,64},{128,96},{160,128},{192,160},{224,192},{256... | collective-permute-start | bytes 147464 | tf_op jit(solution)/shard_map/ppermute | solution.py:15
  399.1 6.7 copy-start.19
  399.1 6.8 copy-start.33
  424.5 272.9 %collective-permute-start.9 = (bf16[2,36,1536]{2,1,0:T(8,128)(2,1)S(1)}, bf16[2,36,1536]{2,1,0:T(8,128)(2,1)S(1)}, u32[]{:S(2)}, u32[]{:S(2)}) collective-permute-start(bf16[2,36,1536]{2,1,0:T(8,128)(2,1)S(1)} %get-tuple-element.13), channel_id=1, source_target_pairs={{0,64},{32,96},{64,128},{96,160},{128,192},{160,224},{192,256},{22... | collective-permute-start | bytes 663560 | tf_op jit(solution)/shard_map/ppermute | solution.py:15
  425.8 271.6 %collective-permute-start.8 = (bf16[2,36,1536]{2,1,0:T(8,128)(2,1)S(1)}, bf16[2,36,1536]{2,1,0:T(8,128)(2,1)S(1)}, u32[]{:S(2)}, u32[]{:S(2)}) collective-permute-start(bf16[2,36,1536]{2,1,0:T(8,128)(2,1)S(1)} %get-tuple-element.13), channel_id=1, source_target_pairs={{0,32},{32,64},{64,96},{96,128},{128,160},{160,192},{192,224},{224... | collective-permute-start | bytes 663560 | tf_op jit(solution)/shard_map/ppermute | solution.py:15
  428.3 269.2 %collective-permute-start.10 = (bf16[2,36,1536]{2,1,0:T(8,128)(2,1)S(1)}, bf16[2,36,1536]{2,1,0:T(8,128)(2,1)S(1)}, u32[]{:S(2)}, u32[]{:S(2)}) collective-permute-start(bf16[2,36,1536]{2,1,0:T(8,128)(2,1)S(1)} %get-tuple-element.14), channel_id=1, source_target_pairs={{32,0},{64,32},{96,64},{128,96},{160,128},{192,160},{224,192},{256... | collective-permute-start | bytes 663560 | tf_op jit(solution)/shard_map/ppermute | solution.py:15
  430.5 267.0 %collective-permute-start.11 = (bf16[2,36,1536]{2,1,0:T(8,128)(2,1)S(1)}, bf16[2,36,1536]{2,1,0:T(8,128)(2,1)S(1)}, u32[]{:S(2)}, u32[]{:S(2)}) collective-permute-start(bf16[2,36,1536]{2,1,0:T(8,128)(2,1)S(1)} %get-tuple-element.14), channel_id=1, source_target_pairs={{64,0},{96,32},{128,64},{160,96},{192,128},{224,160},{256,192},{28... | collective-permute-start | bytes 663560 | tf_op jit(solution)/shard_map/ppermute | solution.py:15
  (28 other events, 77.9 us)
Sparse Core Ops, SparseCore 0:
  140.9 127.6 all-reduce.6
  422.8 271.3 all-reduce.4
where the time goes:
time: 727 us; the launch traced here: 721 us
  waiting for transfers between devices  394 us (54%)
  blocking collectives  90.4 us (12%)
  matrix products  82.1 us (11%)
  local copies, waits for them, and re-layouts  74.7 us (10%)
  starting transfers between devices  33.6 us (5%)
  other arithmetic  27.1 us (4%)
  between operations  19.1 us (3%)
    psum x1, waiting for transfers between devices, local(): summed_dw, summed_pw = lax.psum((grad_dwk, grad_pwk), ('tile', 'img'))  262 us
    psum x1, waiting for transfers between devices, image_total(): summed_states, summed_sums = lax.psum((spread_states, spread_sums), 'tile')  123 us
    psum x2, blocking collectives, image_total(): summed_states, summed_sums = lax.psum((spread_states, spread_sums), 'tile')  90.4 us
    conv_general_dilated x3, matrix products, depthwise(): lax.conv_general_dilated(padded[None], shaped, (1, 1), 'VALID', dimension...  40.4 us
    ppermute x12, starting transfers between devices, from_behind(): lax.ppermute(value, axis, [(source, source + steps) for source in range(i...  33.5 us
    concatenate x9, local copies, waits for them, and re-layouts, local(): jnp.concatenate([grad_queries.reshape(positions, inner_width), grad_keys....  18.2 us
  transfers between devices with their start and end apart: 14, of which 4 were waited for; matrix products, arithmetic and copies ran while one was open for 7% of the time, Pallas kernels for 0%

commit v1 on v0

v1 whole, which is shorter than its diff:
```python
import functools
import math

import jax
import jax.numpy as jnp
from jax import lax
from jax.experimental import pallas as pl
from jax.experimental.pallas import tpu as pltpu
from jax.sharding import PartitionSpec as P

MESH = pl.DeviceIdType.MESH
F32, BF16 = jnp.float32, jnp.bfloat16
EPSILON = 1e-06
TALL, BROAD, LANES, HD = 8, 32, 128, 32
POS = TALL * BROAD
PITCH = 48
NB = 12
TILES = 16
STATE_DT = F32
GRAD_DT = F32


def split(x):
    hi = x.astype(BF16)
    return hi, (x - hi.astype(F32)).astype(BF16)


def dot(a, b, dims):
    return lax.dot_general(a, b, (dims, ((), ())), preferred_element_type=F32)


NN, NT, TN = ((1,), (0,)), ((1,), (1,)), ((0,), (0,))


def mm(a, b, dims):
    out = dot(a[0], b[0], dims)
    if len(b) > 1:
        out = out + dot(a[0], b[1], dims)
    if len(a) > 1:
        out = out + dot(a[1], b[0], dims)
    return out


def kernel(nx, ny, norm, qkv, cot, dw, pw, t_img, t_row, t_col, im_h, im_w, out, gdw, gpw, *scratch):
    (x_raw, x_live, c_in, dwk, pwk, pad, pad2, mix, mrg, gsrc, gmrg, o_blk,
     st_send, st_recv, st_tot, st_out,
     cols_f, corner_f, cols_s, corner_s, rows_s, rows_r, cols_r, corner_r,
     dw_tmp, g_send, g_recv, g_x, g_y, g_tot, g_fin,
     in_sem, out_sem, rs_s, rs_r, ag_s, ag_r, h_s, h_r, gr_s, gr_r, gx_s, gx_r, gy_s, gy_r, ga_s, ga_r) = scratch
    me = lax.axis_index("tile")
    im = lax.axis_index("img")
    mx, my = im // ny, im % ny

    def peer(d):
        return (me + d + TILES) % TILES

    def x_peer(d):
        return ((mx + d) % nx) * ny + my

    def y_peer(d):
        return mx * ny + (my + d) % ny

    def push(src, dst, ssem, rsem, where):
        return pltpu.make_async_remote_copy(
            src_ref=src, dst_ref=dst, send_sem=ssem, recv_sem=rsem, device_id=where, device_id_type=MESH
        )

    def loop(lo, hi, body):
        lax.fori_loop(lo, hi, lambda i, carry: (body(i), carry)[1], 0)

    def in_copies():
        copies = []
        for c in range(NB):
            lanes = pl.ds(c * LANES, LANES)
            copies.append(pltpu.make_async_copy(qkv.at[:, lanes], x_raw.at[c], in_sem.at[c]))
            copies.append(pltpu.make_async_copy(dw.at[:, lanes], dwk.at[c], in_sem.at[NB + c]))
            copies.append(pltpu.make_async_copy(pw.at[:, lanes], pwk.at[c], in_sem.at[2 * NB + c]))
        for c in range(8):
            lanes = pl.ds(c * LANES, LANES)
            copies.append(pltpu.make_async_copy(cot.at[:, lanes], c_in.at[c], in_sem.at[3 * NB + c]))
        return copies

    for copy in in_copies():
        copy.start()

    barrier = pltpu.get_barrier_semaphore()
    loop(1, TILES, lambda d: pl.semaphore_signal(
        barrier, inc=1, device_id={"tile": peer(d)}, device_id_type=MESH))
    if nx > 1:
        loop(1, nx, lambda d: pl.semaphore_signal(
            barrier, inc=1, device_id={"img": x_peer(d)}, device_id_type=MESH))
    if ny > 1:
        loop(1, ny, lambda d: pl.semaphore_signal(
            barrier, inc=1, device_id={"img": y_peer(d)}, device_id_type=MESH))

    slots = im_h.shape[1]
    slot = t_img[0, 0]
    one, zero = jnp.float32(1), jnp.float32(0)

    def flag(cond):
        return jnp.where(cond, one, zero)

    tall, wide, end = jnp.int32(0), jnp.int32(0), jnp.int32(0)
    ends = []
    for m in range(slots):
        tall = tall + jnp.where(slot == m, im_h[0, m], 0)
        wide = wide + jnp.where(slot == m, im_w[0, m], 0)
        end = end + im_h[0, m] * im_w[0, m]
        ends.append(end)
    live = flag(slot < slots)
    has_l = live * flag(t_col[0, 0] > 0)
    has_r = live * flag(t_col[0, 0] < wide - 1)
    has_a = live * flag(t_row[0, 0] > 0)
    has_b = live * flag(t_row[0, 0] < tall - 1)
    thin = flag(wide == 1)
    a1, a2, b1, b2 = has_a * thin, has_a * (one - thin), has_b * thin, has_b * (one - thin)
    keep = [zero] * TILES
    for s in range(1, TILES):
        joined = one
        for m in range(slots):
            joined = joined * flag(ends[m] != s)
        keep[s] = joined

    lane_head = lax.broadcasted_iota(jnp.int32, (LANES, LANES), 1) // HD
    row_head = lax.broadcasted_iota(jnp.int32, (LANES, LANES), 0) // HD
    same_head = flag(lane_head == row_head)
    same_bf = (same_head.astype(BF16),)

    def expand(compact):
        return jnp.concatenate([compact] * 4, axis=0) * same_head

    def compact(full):
        masked = full * same_head
        return masked[0:32] + masked[32:64] + masked[64:96] + masked[96:128]

    def place(c):
        pltpu.make_async_copy(qkv.at[:, pl.ds(0, LANES)], x_raw.at[c], in_sem.at[c]).wait()
        for y in range(TALL):
            rows = x_raw[c, y * BROAD:(y + 1) * BROAD, :].astype(F32) * live
            pad[c, pl.ds((2 + y) * PITCH + 8, BROAD), :] = rows
            x_live[c, y * BROAD:(y + 1) * BROAD, :] = rows.astype(BF16)

    loop(0, NB, place)

    def stage(c, field, k):
        for side, first in ((0, 38), (1, 8)):
            for i in range(2):
                cols_f[i * 8:(i + 1) * 8, :] = field[c, pl.ds(2 * PITCH + first + i, 8, stride=PITCH), :]
            cols_s[k, side, c] = cols_f[...].astype(BF16)

    def stage_corners(field, k):
        for side, row, first in ((0, 8, 38), (1, 2, 8)):
            for c in range(NB):
                for i in range(2):
                    corner_f[4 * c + 2 * i:4 * c + 2 * i + 2, :] = field[c, pl.ds((row + i) * PITCH + first, 2), :]
            corner_s[k, side] = corner_f[...].astype(BF16)

    def halo(k):
        if k == 0:
            bottom, top = x_raw.at[:, pl.ds(POS - 64, 64)], x_raw.at[:, pl.ds(0, 64)]
        else:
            bottom, top = rows_s.at[0], rows_s.at[1]
        plan = [
            (bottom, rows_r.at[k, 0], 1), (top, rows_r.at[k, 1], -1),
            (bottom, rows_r.at[k, 2], 2), (top, rows_r.at[k, 3], -2),
            (cols_s.at[k, 0], cols_r.at[k, 0], 1), (cols_s.at[k, 1], cols_r.at[k, 1], -1),
            (corner_s.at[k, 0], corner_r.at[k, 0], 3), (corner_s.at[k, 1], corner_r.at[k, 1], -3),
        ]
        return [
            push(src, dst, h_s.at[k, i], h_r.at[k, i], {"tile": peer(step)})
            for i, (src, dst, step) in enumerate(plan)
        ]

    def land_corners(field, k):
        for side, row, first, has in ((0, 0, 6, has_a * has_l), (1, 10, 40, has_b * has_r)):
            corner_f[...] = corner_r[k, side].astype(F32) * has
            for c in range(NB):
                for i in range(2):
                    field[c, pl.ds((row + i) * PITCH + first, 2), :] = corner_f[4 * c + 2 * i:4 * c + 2 * i + 2, :]

    def land(c, field, k):
        above1, below1 = rows_r[k, 0, c].astype(F32), rows_r[k, 1, c].astype(F32)
        above2, below2 = rows_r[k, 2, c].astype(F32), rows_r[k, 3, c].astype(F32)
        above = above1 * a1 + above2 * a2
        below = below1 * b1 + below2 * b2
        for i in range(2):
            cut = slice(i * BROAD, (i + 1) * BROAD)
            field[c, pl.ds(i * PITCH + 8, BROAD), :] = above[cut]
            field[c, pl.ds((10 + i) * PITCH + 8, BROAD), :] = below[cut]
            field[c, pl.ds(i * PITCH + 40, 2), :] = above1[i * BROAD:i * BROAD + 2] * (has_a * has_r)
            field[c, pl.ds((10 + i) * PITCH + 6, 2), :] = below1[i * BROAD + 30:i * BROAD + 32] * (has_b * has_l)
        left = cols_r[k, 0, c].astype(F32) * has_l
        right = cols_r[k, 1, c].astype(F32) * has_r
        for i in range(2):
            field[c, pl.ds(2 * PITCH + 6 + i, 8, stride=PITCH), :] = left[i * 8:(i + 1) * 8]
            field[c, pl.ds(2 * PITCH + 40 + i, 8, stride=PITCH), :] = right[i * 8:(i + 1) * 8]

    def convolve(c, field, flipped, put):
        taps = [dwk[c, pl.ds(t, 1), :] for t in range(25)]
        for y in range(0, TALL, 2):
            acc = [None, None]
            for r in range(6):
                for b in range(5):
                    rows = field[c, pl.ds((y + r) * PITCH + 6 + b, BROAD), :]
                    for k in range(2):
                        a = r - k
                        if 0 <= a < 5:
                            t = 24 - (5 * a + b) if flipped else 5 * a + b
                            term = rows * taps[t]
                            acc[k] = term if acc[k] is None else acc[k] + term
            for k in range(2):
                put(c, y + k, acc[k])

    def post_state(e, j, state, key_sum):
        if STATE_DT == F32:
            tail = jnp.broadcast_to(key_sum, (8, LANES))
        else:
            row = lax.broadcasted_iota(jnp.int32, (8, LANES), 0)
            high = key_sum.astype(BF16).astype(F32)
            tail = jnp.where(row == 0, high, jnp.where(row == 1, key_sum - high, 0.0))
        for r in range(4):
            st_send[e, 4 * j + r] = jnp.concatenate([state[8 * r:8 * r + 8], tail], axis=0).astype(STATE_DT)

    def rs(e, d):
        p = peer(d)
        return push(st_send.at[e, p], st_recv.at[e, me], rs_s.at[e, d], rs_r.at[e, me], {"tile": p})

    def rs_from(e, d):
        p = peer(d)
        return push(st_send.at[e, p], st_recv.at[e, p], rs_s.at[e, d], rs_r.at[e, p], {"tile": p})

    def ag(e, d):
        p = peer(d)
        return push(st_tot.at[e, p], st_out.at[e, me], ag_s.at[e, d], ag_r.at[e, me], {"tile": p})

    def ag_from(e, d):
        p = peer(d)
        return push(st_tot.at[e, p], st_out.at[e, p], ag_s.at[e, d], ag_r.at[e, p], {"tile": p})

    def scatter(e):
        loop(1, TILES, lambda d: rs(e, d).start())
        st_recv[e, me] = st_send[e, me]

    def total(e):
        loop(1, TILES, lambda d: rs_from(e, d).wait_recv())
        run = st_recv[e, 0].astype(F32)
        runs = [run]
        for s in range(1, TILES):
            run = run * keep[s] + st_recv[e, s].astype(F32)
            runs.append(run)
        for s in range(TILES - 1, -1, -1):
            if s < TILES - 1:
                run = run * keep[s + 1] + runs[s] * (one - keep[s + 1])
            if STATE_DT == F32:
                st_tot[e, s] = run
            else:
                row = lax.broadcasted_iota(jnp.int32, (8, LANES), 0)
                key_sum = run[8:9] + run[9:10]
                high = key_sum.astype(BF16).astype(F32)
                tail = jnp.where(row == 0, high, jnp.where(row == 1, key_sum - high, 0.0))
                st_tot[e, s] = jnp.concatenate([run[0:8], tail], axis=0).astype(STATE_DT)
        loop(1, TILES, lambda d: ag(e, d).start())
        st_out[e, me] = st_tot[e, me]

    def gather(e):
        loop(1, TILES, lambda d: ag_from(e, d).wait_recv())

    def get_state(e, j):
        parts = [st_out[e, 4 * j + r].astype(F32) for r in range(4)]
        state = expand(jnp.concatenate([part[0:8] for part in parts], axis=0))
        key_sum = parts[0][8:9]
        if STATE_DT != F32:
            key_sum = key_sum + parts[0][9:10]
        return (split(state) if STATE_DT == F32 else (state.astype(BF16),)), key_sum

    def terms(scale, j):
        if scale == 0:
            raw = x_live[j]
            return raw.astype(F32), (raw,)
        raw = mrg[j]
        return raw, split(raw)

    def relu_terms(scale, j):
        raw, parts = terms(scale, j)
        rect = jnp.maximum(raw, 0.0)
        return raw, rect, ((rect.astype(BF16),) if scale == 0 else split(rect))

    def states(scale):
        def body(j):
            _, rect, keys = relu_terms(scale, 4 + j)
            _, values = terms(scale, 8 + j)
            post_state(scale, j, compact(mm(keys, values, TN)), jnp.sum(rect, axis=0, keepdims=True))
        loop(0, 4, body)

    def attend(scale, grads):
        def body(j):
            state, key_sum = get_state(scale, j)
            raw, rect, queries = relu_terms(scale, j)
            den = mm(split(rect * key_sum), same_bf, NN) + EPSILON
            inverse = 1.0 / den
            num = mm(queries, state, NN)
            grad = c_in[4 * scale + j].astype(F32)
            grad_num = grad * inverse
            grad_den = -mm(split(grad_num * num), same_bf, NN) * inverse
            grad_parts = split(grad_num)
            grad_query = mm(grad_parts, state, NT) + grad_den * key_sum
            grads[j] = jnp.where(raw > 0, grad_query, 0.0)
            post_state(2 + scale, j, compact(mm(queries, grad_parts, TN)),
                       jnp.sum(rect * grad_den, axis=0, keepdims=True))
        loop(0, 4, body)

    def attend_back(scale, grads):
        def body(j):
            state, key_sum = get_state(2 + scale, j)
            raw, _, keys = relu_terms(scale, 4 + j)
            _, values = terms(scale, 8 + j)
            grad_key = mm(values, state, NT) + key_sum
            grads[4 + j] = jnp.where(raw > 0, grad_key, 0.0)
            grads[8 + j] = mm(keys, state, NN)
        loop(0, 4, body)

    loop(0, NB, lambda c: stage(c, pad, 0))
    stage_corners(pad, 0)
    states(0)
    pl.semaphore_wait(barrier, (TILES - 1) + (nx - 1) + (ny - 1))
    halo_in = halo(0)
    for copy in halo_in:
        copy.start()
    scatter(0)
    for c in range(NB):
        lanes = pl.ds(c * LANES, LANES)
        pltpu.make_async_copy(dw.at[:, lanes], dwk.at[c], in_sem.at[NB + c]).wait()
        pltpu.make_async_copy(pw.at[:, lanes], pwk.at[c], in_sem.at[2 * NB + c]).wait()
    for c in range(8):
        pltpu.make_async_copy(cot.at[:, pl.ds(c * LANES, LANES)], c_in.at[c], in_sem.at[3 * NB + c]).wait()
    for copy in halo_in:
        copy.wait_recv()
    land_corners(pad, 0)

    def put_mix(c, y, rows):
        mix[c, y * BROAD:(y + 1) * BROAD, :] = rows

    def forward(c):
        land(c, pad, 0)
        convolve(c, pad, False, put_mix)
        weight = split(expand(pwk[c]))
        mrg[c] = mm(split(mix[c]), weight, NN)

    loop(0, NB, forward)
    states(1)
    scatter(1)
    total(0)
    gather(0)
    attend(0, gsrc)
    scatter(2)
    total(1)
    gather(1)
    attend(1, gmrg)
    scatter(3)
    total(2)
    gather(2)
    attend_back(0, gsrc)
    total(3)
    gather(3)
    attend_back(1, gmrg)

    dw_tmp[...] = jnp.zeros((32, LANES), F32)

    def backward(c):
        weight = split(expand(pwk[c]))
        grads = split(gmrg[c] * live)
        grad_mix = mm(grads, weight, NT)
        for y in range(TALL):
            pad2[c, pl.ds((2 + y) * PITCH + 8, BROAD), :] = grad_mix[y * BROAD:(y + 1) * BROAD]
        rows_s[0, c] = grad_mix[POS - 64:].astype(BF16)
        rows_s[1, c] = grad_mix[:64].astype(BF16)
        stage(c, pad2, 1)
        grad_pw = compact(mm(split(mix[c]), grads, TN))
        for b in range(5):
            acc = [None] * 5
            for r in range(12):
                rows = pad[c, pl.ds(r * PITCH + 6 + b, BROAD), :]
                for a in range(5):
                    y = r - a
                    if 0 <= y < TALL:
                        term = rows * pad2[c, pl.ds((2 + y) * PITCH + 8, BROAD), :]
                        acc[a] = term if acc[a] is None else acc[a] + term
            for a in range(5):
                t = 5 * a + b
                dw_tmp[t:t + 1, :] = jnp.sum(acc[a], axis=0, keepdims=True)
        for i in range(2):
            g_send[4 * c + i] = grad_pw[16 * i:16 * i + 16].astype(GRAD_DT)
            g_send[4 * c + 2 + i] = dw_tmp[16 * i:16 * i + 16, :].astype(GRAD_DT)

    loop(0, NB, backward)
    stage_corners(pad2, 1)

    def grad_rs(d):
        p = peer(d)
        return push(g_send.at[pl.ds(3 * p, 3)], g_recv.at[me], gr_s.at[d], gr_r.at[me], {"tile": p})

    def grad_rs_from(d):
        p = peer(d)
        return push(g_send.at[pl.ds(3 * p, 3)], g_recv.at[p], gr_s.at[d], gr_r.at[p], {"tile": p})

    loop(1, TILES, lambda d: grad_rs(d).start())
    g_recv[me] = g_send[pl.ds(3 * me, 3)]
    halo_back = halo(1)
    for copy in halo_back:
        copy.start()

    def add_up(ref, count):
        acc = ref[0].astype(F32)
        for s in range(1, count):
            acc = acc + ref[s].astype(F32)
        return acc

    loop(1, TILES, lambda d: grad_rs_from(d).wait_recv())
    g_x[mx] = add_up(g_recv, TILES)

    def grad_x(d, slot_of):
        return push(g_x.at[mx], g_x.at[slot_of], gx_s.at[d], gx_r.at[slot_of], {"img": x_peer(d)})

    def grad_y(d, slot_of):
        return push(g_y.at[my], g_y.at[slot_of], gy_s.at[d], gy_r.at[slot_of], {"img": y_peer(d)})

    if nx > 1:
        loop(1, nx, lambda d: grad_x(d, mx).start())
    for copy in halo_back:
        copy.wait_recv()
    land_corners(pad2, 1)

    def put_out(c, y, rows):
        rows = (rows + gsrc[c, y * BROAD:(y + 1) * BROAD, :]) * live
        o_blk[c, y * BROAD:(y + 1) * BROAD, :] = rows.astype(BF16)

    def out_copy(c):
        lanes = pl.ds(pl.multiple_of(c * LANES, LANES), LANES)
        return pltpu.make_async_copy(o_blk.at[c], out.at[:, lanes], out_sem.at[c])

    def last(c):
        land(c, pad2, 1)
        convolve(c, pad2, True, put_out)
        out_copy(c).start()

    loop(0, 4, last)
    if nx > 1:
        loop(1, nx, lambda d: grad_x(d, (mx + d) % nx).wait_recv())
    g_y[my] = add_up(g_x, nx)
    if ny > 1:
        loop(1, ny, lambda d: grad_y(d, my).start())
    loop(4, NB, last)
    if ny > 1:
        loop(1, ny, lambda d: grad_y(d, (my + d) % ny).wait_recv())
    g_tot[...] = (add_up(g_y, ny) * norm).astype(GRAD_DT)

    def grad_ag(d, slot_of):
        p = peer(d)
        return push(g_tot, g_fin.at[pl.ds(3 * slot_of, 3)], ga_s.at[d], ga_r.at[slot_of], {"tile": p})

    loop(1, TILES, lambda d: grad_ag(d, me).start())
    g_fin[pl.ds(3 * me, 3)] = g_tot[...]

    for copy in halo_in + halo_back:
        copy.wait_send()

    def drain(d):
        for e in range(4):
            rs(e, d).wait_send()
            ag(e, d).wait_send()
        grad_rs(d).wait_send()

    loop(1, TILES, drain)
    if nx > 1:
        loop(1, nx, lambda d: grad_x(d, mx).wait_send())
    if ny > 1:
        loop(1, ny, lambda d: grad_y(d, my).wait_send())
    loop(0, NB, lambda c: out_copy(c).wait())
    loop(1, TILES, lambda d: grad_ag(d, peer(d)).wait_recv())
    for c in range(NB):
        lanes = slice(c * LANES, (c + 1) * LANES)
        for i in range(2):
            gpw[16 * i:16 * i + 16, lanes] = g_fin[4 * c + i].astype(F32)
        gdw[0:16, lanes] = g_fin[4 * c + 2].astype(F32)
        gdw[16:25, lanes] = g_fin[4 * c + 3].astype(F32)[0:9]
    loop(1, TILES, lambda d: grad_ag(d, me).wait_send())


def local(nx, ny, qkv, cotangent, dw_weight, pw_weight, tile_image, tile_row, tile_col, image_height, image_width):
    channels, inner = qkv.shape[4], cotangent.shape[4]
    norm = 1.0 / math.sqrt(POS * lax.axis_size("tile") * lax.axis_size("img"))
    dma = pltpu.SemaphoreType.DMA
    vm = pltpu.VMEM
    any_spec = pl.BlockSpec(memory_space=pl.ANY)
    smem = pl.BlockSpec(memory_space=pltpu.SMEM)
    vmem = pl.BlockSpec(memory_space=pltpu.VMEM)
    scratch = [
        vm((NB, POS, LANES), BF16), vm((NB, POS, LANES), BF16), vm((8, POS, LANES), BF16),
        vm((NB, 25, LANES), F32), vm((NB, HD, LANES), F32),
        vm((NB, 12 * PITCH, LANES), F32), vm((NB, 12 * PITCH, LANES), F32),
        vm((NB, POS, LANES), F32), vm((NB, POS, LANES), F32), vm((NB, POS, LANES), F32), vm((NB, POS, LANES), F32),
        vm((NB, POS, LANES), BF16),
        vm((4, TILES, 16, LANES), STATE_DT), vm((4, TILES, 16, LANES), STATE_DT),
        vm((4, TILES, 16, LANES), STATE_DT), vm((4, TILES, 16, LANES), STATE_DT),
        vm((16, LANES), F32), vm((48, LANES), F32),
        vm((2, 2, NB, 16, LANES), BF16), vm((2, 2, 48, LANES), BF16), vm((2, NB, 64, LANES), BF16),
        vm((2, 4, NB, 64, LANES), BF16), vm((2, 2, NB, 16, LANES), BF16), vm((2, 2, 48, LANES), BF16),
        vm((32, LANES), F32),
        vm((48, 16, LANES), GRAD_DT), vm((TILES, 3, 16, LANES), GRAD_DT),
        vm((nx, 3, 16, LANES), F32), vm((ny, 3, 16, LANES), F32),
        vm((3, 16, LANES), GRAD_DT), vm((48, 16, LANES), GRAD_DT),
        dma((3 * NB + 8,)), dma((NB,)),
        dma((4, TILES)), dma((4, TILES)), dma((4, TILES)), dma((4, TILES)),
        dma((2, 8)), dma((2, 8)),
        dma((TILES,)), dma((TILES,)), dma((max(nx, 2),)), dma((max(nx, 2),)), dma((max(ny, 2),)), dma((max(ny, 2),)),
        dma((TILES,)), dma((TILES,)),
    ]
    grad, grad_dw, grad_pw = pl.pallas_call(
        functools.partial(kernel, nx, ny, norm),
        out_shape=(
            jax.ShapeDtypeStruct((POS, channels), BF16),
            jax.ShapeDtypeStruct((25, channels), F32),
            jax.ShapeDtypeStruct((HD, channels), F32),
        ),
        in_specs=[any_spec] * 4 + [smem] * 5,
        out_specs=(any_spec, vmem, vmem),
        scratch_shapes=scratch,
        compiler_params=pltpu.CompilerParams(
            collective_id=0, has_side_effects=True, vmem_limit_bytes=60 * 1024 * 1024
        ),
        name="linear_attention",
    )(
        qkv.reshape(POS, channels), cotangent.reshape(POS, inner), dw_weight, pw_weight,
        tile_image, tile_row, tile_col, image_height, image_width,
    )
    return grad.reshape(qkv.shape), grad_dw, grad_pw


def solution(mesh):
    placed = (
        P("img", "tile", None, None, None),
        P("img", "tile", None, None, None),
        P(),
        P(),
        P("img", "tile"),
        P("img", "tile"),
        P("img", "tile"),
        P("img", None),
        P("img", None),
    )
    count = mesh.shape["img"]
    nx = {32: 4, 4: 2}.get(count, 1)
    return jax.shard_map(
        functools.partial(local, nx, count // nx),
        mesh=mesh,
        in_specs=placed,
        out_specs=(P("img", "tile", None, None, None), P(), P()),
        check_vma=False,
    )
```

time: 727 us -> 126 us (0.17)
  waiting for transfers between devices: 394 us -> 0 us
  Pallas kernels: 0 us -> 119 us
  blocking collectives: 90.4 us -> 0 us
  matrix products: 82.1 us -> 0 us
  local copies, waits for them, and re-layouts: 74.7 us -> 3.78 us
  starting transfers between devices: 33.6 us -> 0 us
  other arithmetic: 27.1 us -> 0 us
  between operations: 19.1 us -> 2.59 us
    psum x2 -> x0, waiting for transfers between devices: 385 us -> none  [the longest x1 262 us: local(): summed_dw, summed_pw = lax.psum((grad_dwk, grad_pwk), ('tile', 'img'))]
    pallas_call x0 -> x1, Pallas kernels: none -> 119 us  [local(): pl.pallas_call(functools.partial(kernel, nx, ny, norm), out_shape=(jax.Sh...]
    psum x2 -> x0, blocking collectives: 90.4 us -> none  [image_total(): summed_states, summed_sums = lax.psum((spread_states, spread_sums), 'tile')]
    dot_general x20 -> x0, matrix products: 41.7 us -> none  [the longest x1 6.72 us: block_grad(): jnp.einsum('bgiho,gh->ibho', blocked, jnp.eye(per_block, dtype=jnp.float3...]
    conv_general_dilated x3 -> x0, matrix products: 40.4 us -> none  [depthwise(): lax.conv_general_dilated(padded[None], shaped, (1, 1), 'VALID', dimension...]
    ppermute x12 -> x0, starting transfers between devices: 33.5 us -> none  [from_behind(): lax.ppermute(value, axis, [(source, source + steps) for source in range(i...]
    another operation x17 -> x0, local copies, waits for them, and re-layouts: 19 us -> none  [the longest x1 3.92 us: depthwise(): return result[0]]
    concatenate x9 -> x0, local copies, waits for them, and re-layouts: 18.2 us -> none  [local(): jnp.concatenate([grad_queries.reshape(positions, inner_width), grad_keys....]
  transfers between devices with their start and end apart: 14 -> 0, of which waited for: 4 -> 0; matrix products, arithmetic and copies ran while one was open for 7% -> 0% of each run, Pallas kernels for 0% -> 0%
where the time goes in v1:
time: 126 us
  Pallas kernels  119 us (94%)
  local copies, waits for them, and re-layouts  3.78 us (3%)
  between operations  2.59 us (2%)
    pallas_call x1, Pallas kernels, local(): pl.pallas_call(functools.partial(kernel, nx, ny, norm), out_shape=(jax.Sh...  119 us
    unnamed x7, local copies, waits for them, and re-layouts  3.78 us

profile of v1, /device:TPU:1, one launch (start us, length us, event | category | flops | bytes accessed | tf_op | source)
XLA Modules:
  0.0 125.8 jit_solution(14676239433471803492)
XLA Ops:
  2.6 119.5 %linear_attention.1 = (bf16[256,1536]{1,0:T(8,128)(2,1)}, f32[25,1536]{1,0:T(8,128)}, f32[32,1536]{1,0:T(8,128)}) custom-call(bf16[256,1536]{1,0:T(8,128)(2,1)} %bitcast.3, bf16[256,1024]{1,0:T(8,128)(2,1)} %bitcast.5, f32[25,1536]{1,0:T(8,128)} %dw.1, f32[32,1536]{1,0:T(8,128)} %pw.1, s32[1,1]{1,0:T(1,128)S(6)} %copy.15.t_img, s32[1,1]{1,0:T(1,128)S(6)} %copy.16.t_row, ...), custom_call_target="tpu_custom_call" | custom-call | tf_op jit(solution)/shard_map/linear_attention/pallas_call | solution.py:518
  122.1 0.0 copy-start.1
  122.1 2.1 %copy.18 = bf16[1,1,8,32,1536]{4,3,2,1,0:T(8,128)(2,1)} copy(bf16[1,1,8,32,1536]{4,3,2,1,0:T(8,128)(2,1)} %bitcast.4) | data formatting | bytes 1572864
  124.2 0.0 copy-done.1
  124.2 0.0 copy-start
  124.2 0.7 copy.19
  124.9 0.3 copy-done
  125.2 0.7 copy.20
Async XLA Ops:
  122.1 2.1 %copy-start.1 = (f32[25,1536]{1,0:T(8,128)S(1)}, f32[25,1536]{1,0:T(8,128)}, u32[]{:S(2)}) copy-start(f32[25,1536]{1,0:T(8,128)} %get-tuple-element.13) | copy-start | bytes 460804
  124.2 1.0 copy-start

commit v2 on v1

--- a/solution.py
+++ b/solution.py
@@ -16,8 +16,9 @@
 PITCH = 48
 NB = 12
 TILES = 16
-STATE_DT = F32
-GRAD_DT = F32
+STATE_DT = BF16
+GRAD_DT = BF16
+QB = 4
 
 
 def split(x):
@@ -41,11 +42,11 @@
     return out
 
 
-def kernel(nx, ny, norm, qkv, cot, dw, pw, t_img, t_row, t_col, im_h, im_w, out, gdw, gpw, *scratch):
+def kernel(nx, ny, norm, qkv, cot, dw, pw, t_img, t_row, t_col, im_h, im_w, out, g_fin, *scratch):
     (x_raw, x_live, c_in, dwk, pwk, pad, pad2, mix, mrg, gsrc, gmrg, o_blk,
      st_send, st_recv, st_tot, st_out,
      cols_f, corner_f, cols_s, corner_s, rows_s, rows_r, cols_r, corner_r,
-     dw_tmp, g_send, g_recv, g_x, g_y, g_tot, g_fin,
+     dw_tmp, g_send, g_recv, g_x, g_y, g_tot, g_all,
      in_sem, out_sem, rs_s, rs_r, ag_s, ag_r, h_s, h_r, gr_s, gr_r, gx_s, gx_r, gy_s, gy_r, ga_s, ga_r) = scratch
     me = lax.axis_index("tile")
     im = lax.axis_index("img")
@@ -148,37 +149,40 @@
                 cols_f[i * 8:(i + 1) * 8, :] = field[c, pl.ds(2 * PITCH + first + i, 8, stride=PITCH), :]
             cols_s[k, side, c] = cols_f[...].astype(BF16)
 
-    def stage_corners(field, k):
+    def stage_corners(field, k, lo, hi):
         for side, row, first in ((0, 8, 38), (1, 2, 8)):
-            for c in range(NB):
+            for c in range(lo, hi):
                 for i in range(2):
                     corner_f[4 * c + 2 * i:4 * c + 2 * i + 2, :] = field[c, pl.ds((row + i) * PITCH + first, 2), :]
-            corner_s[k, side] = corner_f[...].astype(BF16)
-
-    def halo(k):
+            corner_s[k, side, 4 * lo:4 * hi] = corner_f[4 * lo:4 * hi, :].astype(BF16)
+
+    def halo(k, lo, hi):
+        blocks, group = pl.ds(lo, hi - lo), int(lo == 0)
+        corner = pl.ds(4 * lo, 4 * (hi - lo))
         if k == 0:
-            bottom, top = x_raw.at[:, pl.ds(POS - 64, 64)], x_raw.at[:, pl.ds(0, 64)]
+            bottom, top = x_raw.at[blocks, pl.ds(POS - 64, 64)], x_raw.at[blocks, pl.ds(0, 64)]
         else:
-            bottom, top = rows_s.at[0], rows_s.at[1]
+            bottom, top = rows_s.at[0, blocks], rows_s.at[1, blocks]
         plan = [
-            (bottom, rows_r.at[k, 0], 1), (top, rows_r.at[k, 1], -1),
-            (bottom, rows_r.at[k, 2], 2), (top, rows_r.at[k, 3], -2),
-            (cols_s.at[k, 0], cols_r.at[k, 0], 1), (cols_s.at[k, 1], cols_r.at[k, 1], -1),
-            (corner_s.at[k, 0], corner_r.at[k, 0], 3), (corner_s.at[k, 1], corner_r.at[k, 1], -3),
+            (cols_s.at[k, 0, blocks], cols_r.at[k, 0, blocks], 1), (cols_s.at[k, 1, blocks], cols_r.at[k, 1, blocks], -1),
+            (corner_s.at[k, 0, corner], corner_r.at[k, 0, corner], 3),
+            (corner_s.at[k, 1, corner], corner_r.at[k, 1, corner], -3),
+            (bottom, rows_r.at[k, 2, blocks], 2), (top, rows_r.at[k, 3, blocks], -2),
+            (bottom, rows_r.at[k, 0, blocks], 1), (top, rows_r.at[k, 1, blocks], -1),
         ]
         return [
-            push(src, dst, h_s.at[k, i], h_r.at[k, i], {"tile": peer(step)})
+            push(src, dst, h_s.at[k, group, i], h_r.at[k, group, i], {"tile": peer(step)})
             for i, (src, dst, step) in enumerate(plan)
         ]
 
-    def land_corners(field, k):
+    def land_corners(field, k, lo, hi):
         for side, row, first, has in ((0, 0, 6, has_a * has_l), (1, 10, 40, has_b * has_r)):
-            corner_f[...] = corner_r[k, side].astype(F32) * has
-            for c in range(NB):
+            corner_f[4 * lo:4 * hi, :] = corner_r[k, side, 4 * lo:4 * hi].astype(F32) * has
+            for c in range(lo, hi):
                 for i in range(2):
                     field[c, pl.ds((row + i) * PITCH + first, 2), :] = corner_f[4 * c + 2 * i:4 * c + 2 * i + 2, :]
 
-    def land(c, field, k):
+    def land_rows(c, field, k):
         above1, below1 = rows_r[k, 0, c].astype(F32), rows_r[k, 1, c].astype(F32)
         above2, below2 = rows_r[k, 2, c].astype(F32), rows_r[k, 3, c].astype(F32)
         above = above1 * a1 + above2 * a2
@@ -189,15 +193,17 @@
             field[c, pl.ds((10 + i) * PITCH + 8, BROAD), :] = below[cut]
             field[c, pl.ds(i * PITCH + 40, 2), :] = above1[i * BROAD:i * BROAD + 2] * (has_a * has_r)
             field[c, pl.ds((10 + i) * PITCH + 6, 2), :] = below1[i * BROAD + 30:i * BROAD + 32] * (has_b * has_l)
+
+    def land_cols(c, field, k):
         left = cols_r[k, 0, c].astype(F32) * has_l
         right = cols_r[k, 1, c].astype(F32) * has_r
         for i in range(2):
             field[c, pl.ds(2 * PITCH + 6 + i, 8, stride=PITCH), :] = left[i * 8:(i + 1) * 8]
             field[c, pl.ds(2 * PITCH + 40 + i, 8, stride=PITCH), :] = right[i * 8:(i + 1) * 8]
 
-    def convolve(c, field, flipped, put):
+    def convolve(c, field, flipped, put, starts):
         taps = [dwk[c, pl.ds(t, 1), :] for t in range(25)]
-        for y in range(0, TALL, 2):
+        for y in starts:
             acc = [None, None]
             for r in range(6):
                 for b in range(5):
@@ -320,49 +326,57 @@
         loop(0, 4, body)
 
     loop(0, NB, lambda c: stage(c, pad, 0))
-    stage_corners(pad, 0)
+    stage_corners(pad, 0, 0, NB)
     states(0)
     pl.semaphore_wait(barrier, (TILES - 1) + (nx - 1) + (ny - 1))
-    halo_in = halo(0)
-    for copy in halo_in:
+    halo_kv, halo_q = halo(0, QB, NB), halo(0, 0, QB)
+    for copy in halo_kv:
         copy.start()
     scatter(0)
+    for copy in halo_q:
+        copy.start()
     for c in range(NB):
         lanes = pl.ds(c * LANES, LANES)
         pltpu.make_async_copy(dw.at[:, lanes], dwk.at[c], in_sem.at[NB + c]).wait()
         pltpu.make_async_copy(pw.at[:, lanes], pwk.at[c], in_sem.at[2 * NB + c]).wait()
     for c in range(8):
         pltpu.make_async_copy(cot.at[:, pl.ds(c * LANES, LANES)], c_in.at[c], in_sem.at[3 * NB + c]).wait()
-    for copy in halo_in:
-        copy.wait_recv()
-    land_corners(pad, 0)
 
     def put_mix(c, y, rows):
         mix[c, y * BROAD:(y + 1) * BROAD, :] = rows
 
-    def forward(c):
-        land(c, pad, 0)
-        convolve(c, pad, False, put_mix)
+    def inner(c):
+        land_cols(c, pad, 0)
+        convolve(c, pad, False, put_mix, (2, 4))
+
+    def outer(c):
+        land_rows(c, pad, 0)
+        convolve(c, pad, False, put_mix, (0, 6))
         weight = split(expand(pwk[c]))
         mrg[c] = mm(split(mix[c]), weight, NN)
 
-    loop(0, NB, forward)
+    for copy in halo_kv[:4]:
+        copy.wait_recv()
+    land_corners(pad, 0, QB, NB)
+    loop(QB, NB, inner)
+    for copy in halo_kv[4:]:
+        copy.wait_recv()
+    loop(QB, NB, outer)
     states(1)
     scatter(1)
     total(0)
+    for copy in halo_q:
+        copy.wait_recv()
+    land_corners(pad, 0, 0, QB)
+    loop(0, QB, lambda c: (inner(c), outer(c)))
+    total(1)
     gather(0)
     attend(0, gsrc)
     scatter(2)
-    total(1)
     gather(1)
     attend(1, gmrg)
     scatter(3)
     total(2)
-    gather(2)
-    attend_back(0, gsrc)
-    total(3)
-    gather(3)
-    attend_back(1, gmrg)
 
     dw_tmp[...] = jnp.zeros((32, LANES), F32)
 
@@ -392,43 +406,75 @@
             g_send[4 * c + i] = grad_pw[16 * i:16 * i + 16].astype(GRAD_DT)
             g_send[4 * c + 2 + i] = dw_tmp[16 * i:16 * i + 16, :].astype(GRAD_DT)
 
-    loop(0, NB, backward)
-    stage_corners(pad2, 1)
-
-    def grad_rs(d):
-        p = peer(d)
-        return push(g_send.at[pl.ds(3 * p, 3)], g_recv.at[me], gr_s.at[d], gr_r.at[me], {"tile": p})
-
-    def grad_rs_from(d):
-        p = peer(d)
-        return push(g_send.at[pl.ds(3 * p, 3)], g_recv.at[p], gr_s.at[d], gr_r.at[p], {"tile": p})
-
-    loop(1, TILES, lambda d: grad_rs(d).start())
-    g_recv[me] = g_send[pl.ds(3 * me, 3)]
-    halo_back = halo(1)
-    for copy in halo_back:
-        copy.start()
-
-    def add_up(ref, count):
-        acc = ref[0].astype(F32)
+    def add_up(ref, count, lo, n):
+        acc = ref[0, lo:lo + n].astype(F32)
         for s in range(1, count):
-            acc = acc + ref[s].astype(F32)
+            acc = acc + ref[s, lo:lo + n].astype(F32)
         return acc
 
-    loop(1, TILES, lambda d: grad_rs_from(d).wait_recv())
-    g_x[mx] = add_up(g_recv, TILES)
-
-    def grad_x(d, slot_of):
-        return push(g_x.at[mx], g_x.at[slot_of], gx_s.at[d], gx_r.at[slot_of], {"img": x_peer(d)})
-
-    def grad_y(d, slot_of):
-        return push(g_y.at[my], g_y.at[slot_of], gy_s.at[d], gy_r.at[slot_of], {"img": y_peer(d)})
-
-    if nx > 1:
-        loop(1, nx, lambda d: grad_x(d, mx).start())
-    for copy in halo_back:
-        copy.wait_recv()
-    land_corners(pad2, 1)
+    class Part:
+        def __init__(self, k, first, lo, n):
+            self.k, self.first, self.lo, self.n = k, first, lo, n
+            self.cut = pl.ds(lo, n)
+
+        def piece(self, p):
+            return pl.ds(self.first + self.n * p, self.n)
+
+        def rs(self, d, slot_of):
+            p = peer(d)
+            return push(g_send.at[self.piece(p)], g_recv.at[slot_of, self.cut],
+                        gr_s.at[self.k, d], gr_r.at[self.k, slot_of], {"tile": p})
+
+        def x(self, d, slot_of):
+            return push(g_x.at[mx, self.cut], g_x.at[slot_of, self.cut],
+                        gx_s.at[self.k, d], gx_r.at[self.k, slot_of], {"img": x_peer(d)})
+
+        def y(self, d, slot_of):
+            return push(g_y.at[my, self.cut], g_y.at[slot_of, self.cut],
+                        gy_s.at[self.k, d], gy_r.at[self.k, slot_of], {"img": y_peer(d)})
+
+        def ag(self, d, slot_of):
+            return push(g_tot.at[self.cut], g_all.at[self.piece(slot_of)],
+                        ga_s.at[self.k, d], ga_r.at[self.k, slot_of], {"tile": peer(d)})
+
+        def scatter(self):
+            loop(1, TILES, lambda d: self.rs(d, me).start())
+            g_recv[me, self.lo:self.lo + self.n] = g_send[self.piece(me)]
+
+        def send_x(self):
+            loop(1, TILES, lambda d: self.rs(d, peer(d)).wait_recv())
+            g_x[mx, self.lo:self.lo + self.n] = add_up(g_recv, TILES, self.lo, self.n)
+            if nx > 1:
+                loop(1, nx, lambda d: self.x(d, mx).start())
+
+        def send_y(self):
+            if nx > 1:
+                loop(1, nx, lambda d: self.x(d, (mx + d) % nx).wait_recv())
+            g_y[my, self.lo:self.lo + self.n] = add_up(g_x, nx, self.lo, self.n)
+            if ny > 1:
+                loop(1, ny, lambda d: self.y(d, my).start())
+
+        def send_all(self):
+            if ny > 1:
+                loop(1, ny, lambda d: self.y(d, (my + d) % ny).wait_recv())
+            g_tot[self.lo:self.lo + self.n] = (add_up(g_y, ny, self.lo, self.n) * norm).astype(GRAD_DT)
+            loop(1, TILES, lambda d: self.ag(d, me).start())
+            g_all[self.piece(me)] = g_tot[self.lo:self.lo + self.n]
+
+        def finish(self):
+            loop(1, TILES, lambda d: self.ag(d, peer(d)).wait_recv())
+
+        def drain(self):
+            def body(d):
+                self.rs(d, me).wait_send()
+                self.ag(d, me).wait_send()
+            loop(1, TILES, body)
+            if nx > 1:
+                loop(1, nx, lambda d: self.x(d, mx).wait_send())
+            if ny > 1:
+                loop(1, ny, lambda d: self.y(d, my).wait_send())
+
+    part_q, part_kv = Part(0, 0, 0, 1), Part(1, 16, 1, 2)
 
     def put_out(c, y, rows):
         rows = (rows + gsrc[c, y * BROAD:(y + 1) * BROAD, :]) * live
@@ -439,51 +485,84 @@
         return pltpu.make_async_copy(o_blk.at[c], out.at[:, lanes], out_sem.at[c])
 
     def last(c):
-        land(c, pad2, 1)
-        convolve(c, pad2, True, put_out)
+        land_cols(c, pad2, 1)
+        land_rows(c, pad2, 1)
+        convolve(c, pad2, True, put_out, (0, 2, 4, 6))
         out_copy(c).start()
 
-    loop(0, 4, last)
-    if nx > 1:
-        loop(1, nx, lambda d: grad_x(d, (mx + d) % nx).wait_recv())
-    g_y[my] = add_up(g_x, nx)
-    if ny > 1:
-        loop(1, ny, lambda d: grad_y(d, my).start())
-    loop(4, NB, last)
-    if ny > 1:
-        loop(1, ny, lambda d: grad_y(d, (my + d) % ny).wait_recv())
-    g_tot[...] = (add_up(g_y, ny) * norm).astype(GRAD_DT)
-
-    def grad_ag(d, slot_of):
-        p = peer(d)
-        return push(g_tot, g_fin.at[pl.ds(3 * slot_of, 3)], ga_s.at[d], ga_r.at[slot_of], {"tile": p})
-
-    loop(1, TILES, lambda d: grad_ag(d, me).start())
-    g_fin[pl.ds(3 * me, 3)] = g_tot[...]
-
-    for copy in halo_in + halo_back:
+    loop(0, QB, backward)
+    part_q.scatter()
+    stage_corners(pad2, 1, 0, QB)
+    back_q = halo(1, 0, QB)
+    for copy in back_q:
+        copy.start()
+    total(3)
+    gather(2)
+    attend_back(0, gsrc)
+    part_q.send_x()
+    for copy in back_q:
+        copy.wait_recv()
+    land_corners(pad2, 1, 0, QB)
+    loop(0, QB, last)
+    gather(3)
+    attend_back(1, gmrg)
+    part_q.send_y()
+    loop(QB, NB, backward)
+    part_kv.scatter()
+    stage_corners(pad2, 1, QB, NB)
+    back_kv = halo(1, QB, NB)
+    for copy in back_kv:
+        copy.start()
+    part_q.send_all()
+    part_kv.send_x()
+    for copy in back_kv:
+        copy.wait_recv()
+    land_corners(pad2, 1, QB, NB)
+    loop(QB, QB + 3, last)
+    part_kv.send_y()
+    loop(QB + 3, NB, last)
+    part_kv.send_all()
+
+    for copy in halo_kv + halo_q + back_q + back_kv:
         copy.wait_send()
 
     def drain(d):
         for e in range(4):
             rs(e, d).wait_send()
             ag(e, d).wait_send()
-        grad_rs(d).wait_send()
 
     loop(1, TILES, drain)
-    if nx > 1:
-        loop(1, nx, lambda d: grad_x(d, mx).wait_send())
-    if ny > 1:
-        loop(1, ny, lambda d: grad_y(d, my).wait_send())
     loop(0, NB, lambda c: out_copy(c).wait())
-    loop(1, TILES, lambda d: grad_ag(d, peer(d)).wait_recv())
+    part_q.finish()
+    part_kv.finish()
+    part_q.drain()
+    part_kv.drain()
+    g_fin[...] = g_all[...]
+
+
+def write(grad, sums, out, gdw, gpw, rows, in_sem, out_sem):
+    steps = 4
+    size = POS // steps
+
+    def take(i):
+        return pltpu.make_async_copy(grad.at[pl.ds(i * size, size)], rows.at[pl.ds(i * size, size)], in_sem.at[i])
+
+    def give(i):
+        return pltpu.make_async_copy(rows.at[pl.ds(i * size, size)], out.at[pl.ds(i * size, size)], out_sem.at[i])
+
+    for i in range(steps):
+        take(i).start()
     for c in range(NB):
         lanes = slice(c * LANES, (c + 1) * LANES)
         for i in range(2):
-            gpw[16 * i:16 * i + 16, lanes] = g_fin[4 * c + i].astype(F32)
-        gdw[0:16, lanes] = g_fin[4 * c + 2].astype(F32)
-        gdw[16:25, lanes] = g_fin[4 * c + 3].astype(F32)[0:9]
-    loop(1, TILES, lambda d: grad_ag(d, me).wait_send())
+            gpw[16 * i:16 * i + 16, lanes] = sums[4 * c + i].astype(F32)
+        gdw[0:16, lanes] = sums[4 * c + 2].astype(F32)
+        gdw[16:25, lanes] = sums[4 * c + 3].astype(F32)[0:9]
+    for i in range(steps):
+        take(i).wait()
+        give(i).start()
+    for i in range(steps):
+        give(i).wait()
 
 
 def local(nx, ny, qkv, cotangent, dw_weight, pw_weight, tile_image, tile_row, tile_col, image_height, image_width):
@@ -511,19 +590,15 @@
         vm((3, 16, LANES), GRAD_DT), vm((48, 16, LANES), GRAD_DT),
         dma((3 * NB + 8,)), dma((NB,)),
         dma((4, TILES)), dma((4, TILES)), dma((4, TILES)), dma((4, TILES)),
-        dma((2, 8)), dma((2, 8)),
-        dma((TILES,)), dma((TILES,)), dma((max(nx, 2),)), dma((max(nx, 2),)), dma((max(ny, 2),)), dma((max(ny, 2),)),
-        dma((TILES,)), dma((TILES,)),
+        dma((2, 2, 8)), dma((2, 2, 8)),
+        dma((2, TILES)), dma((2, TILES)), dma((2, nx)), dma((2, nx)), dma((2, ny)), dma((2, ny)),
+        dma((2, TILES)), dma((2, TILES)),
     ]
-    grad, grad_dw, grad_pw = pl.pallas_call(
+    grad, sums = pl.pallas_call(
         functools.partial(kernel, nx, ny, norm),
-        out_shape=(
-            jax.ShapeDtypeStruct((POS, channels), BF16),
-            jax.ShapeDtypeStruct((25, channels), F32),
-            jax.ShapeDtypeStruct((HD, channels), F32),
-        ),
+        out_shape=(jax.ShapeDtypeStruct((POS, channels), BF16), jax.ShapeDtypeStruct((4 * NB, 16, LANES), GRAD_DT)),
         in_specs=[any_spec] * 4 + [smem] * 5,
-        out_specs=(any_spec, vmem, vmem),
+        out_specs=(any_spec, vmem),
         scratch_shapes=scratch,
         compiler_params=pltpu.CompilerParams(
             collective_id=0, has_side_effects=True, vmem_limit_bytes=60 * 1024 * 1024
@@ -533,6 +608,18 @@
         qkv.reshape(POS, channels), cotangent.reshape(POS, inner), dw_weight, pw_weight,
         tile_image, tile_row, tile_col, image_height, image_width,
     )
+    grad, grad_dw, grad_pw = pl.pallas_call(
+        write,
+        out_shape=(
+            jax.ShapeDtypeStruct((POS, channels), BF16),
+            jax.ShapeDtypeStruct((25, channels), F32),
+            jax.ShapeDtypeStruct((HD, channels), F32),
+        ),
+        in_specs=[any_spec, vmem],
+        out_specs=(any_spec, vmem, vmem),
+        scratch_shapes=[vm((POS, channels), BF16), dma((4,)), dma((4,))],
+        name="write_outputs",
+    )(grad, sums)
     return grad.reshape(qkv.shape), grad_dw, grad_pw
 
 

time: 126 us -> 94.9 us (0.75)
  Pallas kernels: 119 us -> 92 us
  local copies, waits for them, and re-layouts: 3.78 us -> 0 us
    pallas_call x1, Pallas kernels: 119 us -> 88.4 us  [local(): pl.pallas_call(functools.partial(kernel, nx, ny, norm), out_shape=(jax.Sh...]
    unnamed x7 -> x0, local copies, waits for them, and re-layouts: 3.78 us -> none
    pallas_call x0 -> x1, Pallas kernels: none -> 3.63 us  [local(): pl.pallas_call(write, out_shape=(jax.ShapeDtypeStruct((POS, channels), BF...]
where the time goes in v2:
time: 94.9 us; the launch traced here: 94.6 us
  Pallas kernels  92 us (97%)
  between operations  2.58 us (3%)
    pallas_call x1, Pallas kernels, local(): pl.pallas_call(functools.partial(kernel, nx, ny, norm), out_shape=(jax.Sh...  88.4 us
    pallas_call x1, Pallas kernels, local(): pl.pallas_call(write, out_shape=(jax.ShapeDtypeStruct((POS, channels), BF...  3.63 us

profile of v2, /device:TPU:1, one launch (start us, length us, event | category | flops | bytes accessed | tf_op | source)
XLA Modules:
  0.0 94.6 jit_solution(13121721508911196952)
XLA Ops:
  2.6 88.4 %linear_attention.1 = (bf16[256,1536]{1,0:T(8,128)(2,1)}, bf16[48,16,128]{2,1,0:T(8,128)(2,1)}) custom-call(bf16[256,1536]{1,0:T(8,128)(2,1)} %bitcast.3, bf16[256,1024]{1,0:T(8,128)(2,1)} %bitcast.4, f32[25,1536]{1,0:T(8,128)} %dw.1, f32[32,1536]{1,0:T(8,128)} %pw.1, s32[1,1]{1,0:T(1,128)S(6)} %copy.12.t_img, s32[1,1]{1,0:T(1,128)S(6)} %copy.13.t_row, ...), custom_call_target="tpu_custom_call" | custom-call | tf_op jit(solution)/shard_map/linear_attention/pallas_call | solution.py:597
  91.0 3.6 %write_outputs.1 = (bf16[256,1536]{1,0:T(8,128)(2,1)}, f32[25,1536]{1,0:T(8,128)}, f32[32,1536]{1,0:T(8,128)}) custom-call(bf16[256,1536]{1,0:T(8,128)(2,1)} %get-tuple-element.8.grad, bf16[48,16,128]{2,1,0:T(8,128)(2,1)} %get-tuple-element.9.sums), custom_call_target="tpu_custom_call" | custom-call | tf_op jit(solution)/shard_map/write_outputs/pallas_call | solution.py:611

commit v3 on v2

--- a/solution.py
+++ b/solution.py
@@ -42,12 +42,12 @@
     return out
 
 
-def kernel(nx, ny, norm, qkv, cot, dw, pw, t_img, t_row, t_col, im_h, im_w, out, g_fin, *scratch):
-    (x_raw, x_live, c_in, dwk, pwk, pad, pad2, mix, mrg, gsrc, gmrg, o_blk,
+def kernel(nx, ny, norm, qkv, cot, dw, pw, im_h_in, im_w_in, out, g_fin, *scratch):
+    (x_raw, c_in, dwk, pwk, pad, pad2, mix, mrg, gsrc, gmrg, im_h, im_w,
      st_send, st_recv, st_tot, st_out,
      cols_f, corner_f, cols_s, corner_s, rows_s, rows_r, cols_r, corner_r,
      dw_tmp, g_send, g_recv, g_x, g_y, g_tot, g_all,
-     in_sem, out_sem, rs_s, rs_r, ag_s, ag_r, h_s, h_r, gr_s, gr_r, gx_s, gx_r, gy_s, gy_r, ga_s, ga_r) = scratch
+     in_sem, meta_sem, rs_s, rs_r, ag_s, ag_r, h_s, h_r, gr_s, gr_r, gx_s, gx_r, gy_s, gy_r, ga_s, ga_r) = scratch
     me = lax.axis_index("tile")
     im = lax.axis_index("img")
     mx, my = im // ny, im % ny
@@ -68,6 +68,9 @@
 
     def loop(lo, hi, body):
         lax.fori_loop(lo, hi, lambda i, carry: (body(i), carry)[1], 0)
+
+    def far_first(count, body):
+        loop(0, count - 1, lambda i: body(count // 2 + ((i + 1) // 2) * (1 - 2 * (i % 2))))
 
     def in_copies():
         copies = []
@@ -81,46 +84,28 @@
             copies.append(pltpu.make_async_copy(cot.at[:, lanes], c_in.at[c], in_sem.at[3 * NB + c]))
         return copies
 
-    for copy in in_copies():
+    meta = [
+        pltpu.make_async_copy(src, dst, meta_sem.at[i])
+        for i, (src, dst) in enumerate(
+            ((im_h_in, im_h), (im_w_in, im_w)))
+    ]
+    for copy in meta + in_copies():
         copy.start()
 
     barrier = pltpu.get_barrier_semaphore()
-    loop(1, TILES, lambda d: pl.semaphore_signal(
+    far_first(TILES, lambda d: pl.semaphore_signal(
         barrier, inc=1, device_id={"tile": peer(d)}, device_id_type=MESH))
     if nx > 1:
-        loop(1, nx, lambda d: pl.semaphore_signal(
+        far_first(nx, lambda d: pl.semaphore_signal(
             barrier, inc=1, device_id={"img": x_peer(d)}, device_id_type=MESH))
     if ny > 1:
-        loop(1, ny, lambda d: pl.semaphore_signal(
+        far_first(ny, lambda d: pl.semaphore_signal(
             barrier, inc=1, device_id={"img": y_peer(d)}, device_id_type=MESH))
 
-    slots = im_h.shape[1]
-    slot = t_img[0, 0]
     one, zero = jnp.float32(1), jnp.float32(0)
 
     def flag(cond):
         return jnp.where(cond, one, zero)
-
-    tall, wide, end = jnp.int32(0), jnp.int32(0), jnp.int32(0)
-    ends = []
-    for m in range(slots):
-        tall = tall + jnp.where(slot == m, im_h[0, m], 0)
-        wide = wide + jnp.where(slot == m, im_w[0, m], 0)
-        end = end + im_h[0, m] * im_w[0, m]
-        ends.append(end)
-    live = flag(slot < slots)
-    has_l = live * flag(t_col[0, 0] > 0)
-    has_r = live * flag(t_col[0, 0] < wide - 1)
-    has_a = live * flag(t_row[0, 0] > 0)
-    has_b = live * flag(t_row[0, 0] < tall - 1)
-    thin = flag(wide == 1)
-    a1, a2, b1, b2 = has_a * thin, has_a * (one - thin), has_b * thin, has_b * (one - thin)
-    keep = [zero] * TILES
-    for s in range(1, TILES):
-        joined = one
-        for m in range(slots):
-            joined = joined * flag(ends[m] != s)
-        keep[s] = joined
 
     lane_head = lax.broadcasted_iota(jnp.int32, (LANES, LANES), 1) // HD
     row_head = lax.broadcasted_iota(jnp.int32, (LANES, LANES), 0) // HD
@@ -137,9 +122,8 @@
     def place(c):
         pltpu.make_async_copy(qkv.at[:, pl.ds(0, LANES)], x_raw.at[c], in_sem.at[c]).wait()
         for y in range(TALL):
-            rows = x_raw[c, y * BROAD:(y + 1) * BROAD, :].astype(F32) * live
+            rows = x_raw[c, y * BROAD:(y + 1) * BROAD, :].astype(F32)
             pad[c, pl.ds((2 + y) * PITCH + 8, BROAD), :] = rows
-            x_live[c, y * BROAD:(y + 1) * BROAD, :] = rows.astype(BF16)
 
     loop(0, NB, place)
 
@@ -157,7 +141,7 @@
             corner_s[k, side, 4 * lo:4 * hi] = corner_f[4 * lo:4 * hi, :].astype(BF16)
 
     def halo(k, lo, hi):
-        blocks, group = pl.ds(lo, hi - lo), int(lo == 0)
+        blocks, group = pl.ds(lo, hi - lo), lo // QB
         corner = pl.ds(4 * lo, 4 * (hi - lo))
         if k == 0:
             bottom, top = x_raw.at[blocks, pl.ds(POS - 64, 64)], x_raw.at[blocks, pl.ds(0, 64)]
@@ -244,19 +228,18 @@
         return push(st_tot.at[e, p], st_out.at[e, p], ag_s.at[e, d], ag_r.at[e, p], {"tile": p})
 
     def scatter(e):
-        loop(1, TILES, lambda d: rs(e, d).start())
+        far_first(TILES, lambda d: rs(e, d).start())
         st_recv[e, me] = st_send[e, me]
 
     def total(e):
         loop(1, TILES, lambda d: rs_from(e, d).wait_recv())
-        run = st_recv[e, 0].astype(F32)
-        runs = [run]
+        part = [st_recv[e, s].astype(F32) for s in range(TILES)]
+        ahead, behind = [part[0]], [jnp.zeros_like(part[0])]
         for s in range(1, TILES):
-            run = run * keep[s] + st_recv[e, s].astype(F32)
-            runs.append(run)
-        for s in range(TILES - 1, -1, -1):
-            if s < TILES - 1:
-                run = run * keep[s + 1] + runs[s] * (one - keep[s + 1])
+            ahead.append(ahead[-1] * keep[s] + part[s])
+            behind.append((behind[-1] + part[TILES - s]) * keep[TILES - s])
+        for s in range(TILES):
+            run = ahead[s] + behind[TILES - 1 - s]
             if STATE_DT == F32:
                 st_tot[e, s] = run
             else:
@@ -265,7 +248,7 @@
                 high = key_sum.astype(BF16).astype(F32)
                 tail = jnp.where(row == 0, high, jnp.where(row == 1, key_sum - high, 0.0))
                 st_tot[e, s] = jnp.concatenate([run[0:8], tail], axis=0).astype(STATE_DT)
-        loop(1, TILES, lambda d: ag(e, d).start())
+        far_first(TILES, lambda d: ag(e, d).start())
         st_out[e, me] = st_tot[e, me]
 
     def gather(e):
@@ -281,7 +264,7 @@
 
     def terms(scale, j):
         if scale == 0:
-            raw = x_live[j]
+            raw = x_raw[j]
             return raw.astype(F32), (raw,)
         raw = mrg[j]
         return raw, split(raw)
@@ -327,14 +310,45 @@
 
     loop(0, NB, lambda c: stage(c, pad, 0))
     stage_corners(pad, 0, 0, NB)
+    pl.semaphore_wait(barrier, (TILES - 1) + (nx - 1) + (ny - 1))
+    halo_q, halo_k, halo_v = (halo(0, lo, lo + QB) for lo in (0, QB, 2 * QB))
+    for copy in halo_k[:4] + halo_v[:4] + halo_k[4:] + halo_v[4:]:
+        copy.start()
     states(0)
-    pl.semaphore_wait(barrier, (TILES - 1) + (nx - 1) + (ny - 1))
-    halo_kv, halo_q = halo(0, QB, NB), halo(0, 0, QB)
-    for copy in halo_kv:
-        copy.start()
     scatter(0)
     for copy in halo_q:
         copy.start()
+
+    for copy in meta:
+        copy.wait()
+    slots = im_h.shape[1]
+    tall, wide, first, end = (jnp.int32(0) for _ in range(4))
+    ends = []
+    for m in range(slots):
+        start = end
+        end = end + im_h[0, m] * im_w[0, m]
+        mine = (start <= me) & (me < end)
+        tall = tall + jnp.where(mine, im_h[0, m], 0)
+        wide = wide + jnp.where(mine, im_w[0, m], 0)
+        first = first + jnp.where(mine, start, 0)
+        ends.append(end)
+    live = flag(me < end)
+    within = me - first
+    col = jnp.where(wide == 2, within % 2, 0)
+    row = jnp.where(wide == 2, within // 2, within)
+    has_l = live * flag(col > 0)
+    has_r = live * flag(col < wide - 1)
+    has_a = live * flag(row > 0)
+    has_b = live * flag(row < tall - 1)
+    thin = flag(wide == 1)
+    a1, a2, b1, b2 = has_a * thin, has_a * (one - thin), has_b * thin, has_b * (one - thin)
+    keep = [zero] * TILES
+    for s in range(1, TILES):
+        joined = one
+        for m in range(slots):
+            joined = joined * flag(ends[m] != s)
+        keep[s] = joined
+
     for c in range(NB):
         lanes = pl.ds(c * LANES, LANES)
         pltpu.make_async_copy(dw.at[:, lanes], dwk.at[c], in_sem.at[NB + c]).wait()
@@ -355,13 +369,16 @@
         weight = split(expand(pwk[c]))
         mrg[c] = mm(split(mix[c]), weight, NN)
 
-    for copy in halo_kv[:4]:
+    for copy in halo_k[:4] + halo_v[:4]:
         copy.wait_recv()
     land_corners(pad, 0, QB, NB)
     loop(QB, NB, inner)
-    for copy in halo_kv[4:]:
+    for copy in halo_k[4:]:
         copy.wait_recv()
-    loop(QB, NB, outer)
+    loop(QB, 2 * QB, outer)
+    for copy in halo_v[4:]:
+        copy.wait_recv()
+    loop(2 * QB, NB, outer)
     states(1)
     scatter(1)
     total(0)
@@ -398,6 +415,7 @@
                     y = r - a
                     if 0 <= y < TALL:
                         term = rows * pad2[c, pl.ds((2 + y) * PITCH + 8, BROAD), :]
+                        term = (term[0:8] + term[8:16]) + (term[16:24] + term[24:32])
                         acc[a] = term if acc[a] is None else acc[a] + term
             for a in range(5):
                 t = 5 * a + b
@@ -438,27 +456,27 @@
                         ga_s.at[self.k, d], ga_r.at[self.k, slot_of], {"tile": peer(d)})
 
         def scatter(self):
-            loop(1, TILES, lambda d: self.rs(d, me).start())
+            far_first(TILES, lambda d: self.rs(d, me).start())
             g_recv[me, self.lo:self.lo + self.n] = g_send[self.piece(me)]
 
         def send_x(self):
             loop(1, TILES, lambda d: self.rs(d, peer(d)).wait_recv())
             g_x[mx, self.lo:self.lo + self.n] = add_up(g_recv, TILES, self.lo, self.n)
             if nx > 1:
-                loop(1, nx, lambda d: self.x(d, mx).start())
+                far_first(nx, lambda d: self.x(d, mx).start())
 
         def send_y(self):
             if nx > 1:
                 loop(1, nx, lambda d: self.x(d, (mx + d) % nx).wait_recv())
             g_y[my, self.lo:self.lo + self.n] = add_up(g_x, nx, self.lo, self.n)
             if ny > 1:
-                loop(1, ny, lambda d: self.y(d, my).start())
+                far_first(ny, lambda d: self.y(d, my).start())
 
         def send_all(self):
             if ny > 1:
                 loop(1, ny, lambda d: self.y(d, (my + d) % ny).wait_recv())
             g_tot[self.lo:self.lo + self.n] = (add_up(g_y, ny, self.lo, self.n) * norm).astype(GRAD_DT)
-            loop(1, TILES, lambda d: self.ag(d, me).start())
+            far_first(TILES, lambda d: self.ag(d, me).start())
             g_all[self.piece(me)] = g_tot[self.lo:self.lo + self.n]
 
         def finish(self):
@@ -474,56 +492,59 @@
             if ny > 1:
                 loop(1, ny, lambda d: self.y(d, my).wait_send())
 
-    part_q, part_kv = Part(0, 0, 0, 1), Part(1, 16, 1, 2)
+    part_q, part_k, part_v = (Part(k, 16 * k, k, 1) for k in range(3))
 
     def put_out(c, y, rows):
         rows = (rows + gsrc[c, y * BROAD:(y + 1) * BROAD, :]) * live
-        o_blk[c, y * BROAD:(y + 1) * BROAD, :] = rows.astype(BF16)
-
-    def out_copy(c):
         lanes = pl.ds(pl.multiple_of(c * LANES, LANES), LANES)
-        return pltpu.make_async_copy(o_blk.at[c], out.at[:, lanes], out_sem.at[c])
+        out[y * BROAD:(y + 1) * BROAD, lanes] = rows.astype(BF16)
 
     def last(c):
         land_cols(c, pad2, 1)
         land_rows(c, pad2, 1)
         convolve(c, pad2, True, put_out, (0, 2, 4, 6))
-        out_copy(c).start()
+
+    back_q, back_k, back_v = (halo(1, lo, lo + QB) for lo in (0, QB, 2 * QB))
+
+    def send_back(copies, lo):
+        stage_corners(pad2, 1, lo, lo + QB)
+        for copy in copies:
+            copy.start()
+
+    def finish_back(copies, lo):
+        for copy in copies:
+            copy.wait_recv()
+        land_corners(pad2, 1, lo, lo + QB)
+        loop(lo, lo + QB, last)
 
     loop(0, QB, backward)
     part_q.scatter()
-    stage_corners(pad2, 1, 0, QB)
-    back_q = halo(1, 0, QB)
-    for copy in back_q:
-        copy.start()
     total(3)
+    send_back(back_q, 0)
     gather(2)
     attend_back(0, gsrc)
     part_q.send_x()
-    for copy in back_q:
-        copy.wait_recv()
-    land_corners(pad2, 1, 0, QB)
-    loop(0, QB, last)
     gather(3)
     attend_back(1, gmrg)
     part_q.send_y()
-    loop(QB, NB, backward)
-    part_kv.scatter()
-    stage_corners(pad2, 1, QB, NB)
-    back_kv = halo(1, QB, NB)
-    for copy in back_kv:
-        copy.start()
+    loop(QB, 2 * QB, backward)
+    part_k.scatter()
+    loop(2 * QB, NB, backward)
+    part_v.scatter()
+    send_back(back_k, QB)
+    send_back(back_v, 2 * QB)
+    part_k.send_x()
     part_q.send_all()
-    part_kv.send_x()
-    for copy in back_kv:
-        copy.wait_recv()
-    land_corners(pad2, 1, QB, NB)
-    loop(QB, QB + 3, last)
-    part_kv.send_y()
-    loop(QB + 3, NB, last)
-    part_kv.send_all()
-
-    for copy in halo_kv + halo_q + back_q + back_kv:
+    finish_back(back_q, 0)
+    part_v.send_x()
+    part_k.send_y()
+    finish_back(back_k, QB)
+    part_v.send_y()
+    finish_back(back_v, 2 * QB)
+    part_k.send_all()
+    part_v.send_all()
+
+    for copy in halo_q + halo_k + halo_v + back_q + back_k + back_v:
         copy.wait_send()
 
     def drain(d):
@@ -532,37 +553,23 @@
             ag(e, d).wait_send()
 
     loop(1, TILES, drain)
-    loop(0, NB, lambda c: out_copy(c).wait())
-    part_q.finish()
-    part_kv.finish()
-    part_q.drain()
-    part_kv.drain()
+    for part in (part_q, part_k, part_v):
+        part.finish()
+    for part in (part_q, part_k, part_v):
+        part.drain()
     g_fin[...] = g_all[...]
 
 
-def write(grad, sums, out, gdw, gpw, rows, in_sem, out_sem):
-    steps = 4
-    size = POS // steps
-
-    def take(i):
-        return pltpu.make_async_copy(grad.at[pl.ds(i * size, size)], rows.at[pl.ds(i * size, size)], in_sem.at[i])
-
-    def give(i):
-        return pltpu.make_async_copy(rows.at[pl.ds(i * size, size)], out.at[pl.ds(i * size, size)], out_sem.at[i])
-
-    for i in range(steps):
-        take(i).start()
+def write(grad, sums, out, gdw, gpw, out_sem):
+    copy = pltpu.make_async_copy(grad, out, out_sem)
+    copy.start()
     for c in range(NB):
         lanes = slice(c * LANES, (c + 1) * LANES)
         for i in range(2):
             gpw[16 * i:16 * i + 16, lanes] = sums[4 * c + i].astype(F32)
         gdw[0:16, lanes] = sums[4 * c + 2].astype(F32)
         gdw[16:25, lanes] = sums[4 * c + 3].astype(F32)[0:9]
-    for i in range(steps):
-        take(i).wait()
-        give(i).start()
-    for i in range(steps):
-        give(i).wait()
+    copy.wait()
 
 
 def local(nx, ny, qkv, cotangent, dw_weight, pw_weight, tile_image, tile_row, tile_col, image_height, image_width):
@@ -570,15 +577,14 @@
     norm = 1.0 / math.sqrt(POS * lax.axis_size("tile") * lax.axis_size("img"))
     dma = pltpu.SemaphoreType.DMA
     vm = pltpu.VMEM
-    any_spec = pl.BlockSpec(memory_space=pl.ANY)
-    smem = pl.BlockSpec(memory_space=pltpu.SMEM)
+    hbm_spec = pl.BlockSpec(memory_space=pltpu.HBM)
     vmem = pl.BlockSpec(memory_space=pltpu.VMEM)
     scratch = [
-        vm((NB, POS, LANES), BF16), vm((NB, POS, LANES), BF16), vm((8, POS, LANES), BF16),
+        vm((NB, POS, LANES), BF16), vm((8, POS, LANES), BF16),
         vm((NB, 25, LANES), F32), vm((NB, HD, LANES), F32),
         vm((NB, 12 * PITCH, LANES), F32), vm((NB, 12 * PITCH, LANES), F32),
         vm((NB, POS, LANES), F32), vm((NB, POS, LANES), F32), vm((NB, POS, LANES), F32), vm((NB, POS, LANES), F32),
-        vm((NB, POS, LANES), BF16),
+        pltpu.SMEM(image_height.shape, jnp.int32), pltpu.SMEM(image_width.shape, jnp.int32),
         vm((4, TILES, 16, LANES), STATE_DT), vm((4, TILES, 16, LANES), STATE_DT),
         vm((4, TILES, 16, LANES), STATE_DT), vm((4, TILES, 16, LANES), STATE_DT),
         vm((16, LANES), F32), vm((48, LANES), F32),
@@ -588,25 +594,26 @@
         vm((48, 16, LANES), GRAD_DT), vm((TILES, 3, 16, LANES), GRAD_DT),
         vm((nx, 3, 16, LANES), F32), vm((ny, 3, 16, LANES), F32),
         vm((3, 16, LANES), GRAD_DT), vm((48, 16, LANES), GRAD_DT),
-        dma((3 * NB + 8,)), dma((NB,)),
+        dma((3 * NB + 8,)), dma((2,)),
         dma((4, TILES)), dma((4, TILES)), dma((4, TILES)), dma((4, TILES)),
-        dma((2, 2, 8)), dma((2, 2, 8)),
-        dma((2, TILES)), dma((2, TILES)), dma((2, nx)), dma((2, nx)), dma((2, ny)), dma((2, ny)),
-        dma((2, TILES)), dma((2, TILES)),
+        dma((2, 3, 8)), dma((2, 3, 8)),
+        dma((3, TILES)), dma((3, TILES)), dma((3, nx)), dma((3, nx)), dma((3, ny)), dma((3, ny)),
+        dma((3, TILES)), dma((3, TILES)),
     ]
     grad, sums = pl.pallas_call(
         functools.partial(kernel, nx, ny, norm),
         out_shape=(jax.ShapeDtypeStruct((POS, channels), BF16), jax.ShapeDtypeStruct((4 * NB, 16, LANES), GRAD_DT)),
-        in_specs=[any_spec] * 4 + [smem] * 5,
-        out_specs=(any_spec, vmem),
+        in_specs=[hbm_spec] * 6,
+        out_specs=(vmem, vmem),
         scratch_shapes=scratch,
         compiler_params=pltpu.CompilerParams(
-            collective_id=0, has_side_effects=True, vmem_limit_bytes=60 * 1024 * 1024
+            collective_id=0, has_side_effects=True, vmem_limit_bytes=40 * 1024 * 1024
         ),
         name="linear_attention",
     )(
-        qkv.reshape(POS, channels), cotangent.reshape(POS, inner), dw_weight, pw_weight,
-        tile_image, tile_row, tile_col, image_height, image_width,
+        *[pltpu.with_memory_space_constraint(x, pltpu.HBM) for x in (
+            qkv.reshape(POS, channels), cotangent.reshape(POS, inner), dw_weight, pw_weight,
+            image_height, image_width)]
     )
     grad, grad_dw, grad_pw = pl.pallas_call(
         write,
@@ -615,9 +622,10 @@
             jax.ShapeDtypeStruct((25, channels), F32),
             jax.ShapeDtypeStruct((HD, channels), F32),
         ),
-        in_specs=[any_spec, vmem],
-        out_specs=(any_spec, vmem, vmem),
-        scratch_shapes=[vm((POS, channels), BF16), dma((4,)), dma((4,))],
+        in_specs=[vmem, vmem],
+        out_specs=(hbm_spec, vmem, vmem),
+        scratch_shapes=[dma(())],
+        compiler_params=pltpu.CompilerParams(vmem_limit_bytes=8 * 1024 * 1024),
         name="write_outputs",
     )(grad, sums)
     return grad.reshape(qkv.shape), grad_dw, grad_pw

time: 94.9 us -> 80.7 us (0.85)
  Pallas kernels: 92 us -> 79.9 us
  between operations: 2.58 us -> 0.64 us
    pallas_call x1, Pallas kernels: 88.4 us -> 78.3 us  [local(): pl.pallas_call(functools.partial(kernel, nx, ny, norm), out_shape=(jax.Sh...]
    pallas_call x1, Pallas kernels: 3.63 us -> 1.63 us  [local(): pl.pallas_call(write, out_shape=(jax.ShapeDtypeStruct((POS, channels), BF...]
where the time goes in v3:
time: 80.7 us; the launch traced here: 80.5 us
  Pallas kernels  79.9 us (99%)
    pallas_call x1, Pallas kernels, local(): pl.pallas_call(functools.partial(kernel, nx, ny, norm), out_shape=(jax.Sh...  78.3 us
    pallas_call x1, Pallas kernels, local(): pl.pallas_call(write, out_shape=(jax.ShapeDtypeStruct((POS, channels), BF...  1.63 us

profile of v3, /device:TPU:1, one launch (start us, length us, event | category | flops | bytes accessed | tf_op | source)
XLA Modules:
  0.0 80.5 jit_solution(17563570017006430709)
XLA Ops:
  0.6 78.3 %linear_attention.1 = (bf16[256,1536]{1,0:T(8,128)(2,1)S(1)}, bf16[48,16,128]{2,1,0:T(8,128)(2,1)S(1)}) custom-call(bf16[256,1536]{1,0:T(8,128)(2,1)} %bitcast.3, bf16[256,1024]{1,0:T(8,128)(2,1)} %bitcast.4, f32[25,1536]{1,0:T(8,128)} %dw.1, f32[32,1536]{1,0:T(8,128)} %pw.1, s32[1,8]{1,0:T(1,128)} %im_h_in.1, s32[1,8]{1,0:T(1,128)} %im_w_in.1), custom_call_target="tpu_custom_call" | custom-call | tf_op jit(solution)/shard_map/linear_attention/pallas_call | solution.py:603
  78.9 1.6 %write_outputs.1 = (bf16[256,1536]{1,0:T(8,128)(2,1)}, f32[25,1536]{1,0:T(8,128)}, f32[32,1536]{1,0:T(8,128)}) custom-call(bf16[256,1536]{1,0:T(8,128)(2,1)S(1)} %get-tuple-element.8.grad, bf16[48,16,128]{2,1,0:T(8,128)(2,1)S(1)} %get-tuple-element.9.sums), custom_call_target="tpu_custom_call" | custom-call | tf_op jit(solution)/shard_map/write_outputs/pallas_call | solution.py:618

commit v4 on v3

--- a/solution.py
+++ b/solution.py
@@ -43,23 +43,23 @@
 
 
 def kernel(nx, ny, norm, qkv, cot, dw, pw, im_h_in, im_w_in, out, g_fin, *scratch):
-    (x_raw, c_in, dwk, pwk, pad, pad2, mix, mrg, gsrc, gmrg, im_h, im_w,
+    (x_raw, c_in, m_hi, m_lo, w_hi, w_lo, dwk, pwk, pad, pad2, mix, mrg, gsrc, gmrg, im_h, im_w,
      st_send, st_recv, st_tot, st_out,
      cols_f, corner_f, cols_s, corner_s, rows_s, rows_r, cols_r, corner_r,
      dw_tmp, g_send, g_recv, g_x, g_y, g_tot, g_all,
      in_sem, meta_sem, rs_s, rs_r, ag_s, ag_r, h_s, h_r, gr_s, gr_r, gx_s, gx_r, gy_s, gy_r, ga_s, ga_r) = scratch
     me = lax.axis_index("tile")
     im = lax.axis_index("img")
-    mx, my = im // ny, im % ny
+    mx, my = lax.div(im, ny), lax.rem(im, ny)
 
     def peer(d):
-        return (me + d + TILES) % TILES
+        return lax.rem(me + (d + TILES), TILES)
 
     def x_peer(d):
-        return ((mx + d) % nx) * ny + my
+        return lax.rem(mx + d, nx) * ny + my
 
     def y_peer(d):
-        return mx * ny + (my + d) % ny
+        return mx * ny + lax.rem(my + d, ny)
 
     def push(src, dst, ssem, rsem, where):
         return pltpu.make_async_remote_copy(
@@ -70,15 +70,19 @@
         lax.fori_loop(lo, hi, lambda i, carry: (body(i), carry)[1], 0)
 
     def far_first(count, body):
-        loop(0, count - 1, lambda i: body(count // 2 + ((i + 1) // 2) * (1 - 2 * (i % 2))))
+        half = count // 2
+        body(half)
+        loop(1, half, lambda h: (body(half - h), body(half + h)))
 
     def in_copies():
         copies = []
         for c in range(NB):
             lanes = pl.ds(c * LANES, LANES)
             copies.append(pltpu.make_async_copy(qkv.at[:, lanes], x_raw.at[c], in_sem.at[c]))
+        for c in range(NB):
+            lanes = pl.ds(c * LANES, LANES)
+            copies.append(pltpu.make_async_copy(pw.at[:, lanes], pwk.at[c], in_sem.at[2 * NB + c]))
             copies.append(pltpu.make_async_copy(dw.at[:, lanes], dwk.at[c], in_sem.at[NB + c]))
-            copies.append(pltpu.make_async_copy(pw.at[:, lanes], pwk.at[c], in_sem.at[2 * NB + c]))
         for c in range(8):
             lanes = pl.ds(c * LANES, LANES)
             copies.append(pltpu.make_async_copy(cot.at[:, lanes], c_in.at[c], in_sem.at[3 * NB + c]))
@@ -366,9 +370,13 @@
     def outer(c):
         land_rows(c, pad, 0)
         convolve(c, pad, False, put_mix, (0, 6))
-        weight = split(expand(pwk[c]))
-        mrg[c] = mm(split(mix[c]), weight, NN)
-
+        m_hi[c], m_lo[c] = split(mix[c])
+        mrg[c] = mm((m_hi[c], m_lo[c]), (w_hi[c], w_lo[c]), NN)
+
+    def weigh(c):
+        w_hi[c], w_lo[c] = split(expand(pwk[c]))
+
+    loop(0, NB, weigh)
     for copy in halo_k[:4] + halo_v[:4]:
         copy.wait_recv()
     land_corners(pad, 0, QB, NB)
@@ -398,15 +406,14 @@
     dw_tmp[...] = jnp.zeros((32, LANES), F32)
 
     def backward(c):
-        weight = split(expand(pwk[c]))
         grads = split(gmrg[c] * live)
-        grad_mix = mm(grads, weight, NT)
+        grad_mix = mm(grads, (w_hi[c], w_lo[c]), NT)
         for y in range(TALL):
             pad2[c, pl.ds((2 + y) * PITCH + 8, BROAD), :] = grad_mix[y * BROAD:(y + 1) * BROAD]
         rows_s[0, c] = grad_mix[POS - 64:].astype(BF16)
         rows_s[1, c] = grad_mix[:64].astype(BF16)
         stage(c, pad2, 1)
-        grad_pw = compact(mm(split(mix[c]), grads, TN))
+        grad_pw = compact(mm((m_hi[c], m_lo[c]), grads, TN))
         for b in range(5):
             acc = [None] * 5
             for r in range(12):
@@ -467,14 +474,14 @@
 
         def send_y(self):
             if nx > 1:
-                loop(1, nx, lambda d: self.x(d, (mx + d) % nx).wait_recv())
-            g_y[my, self.lo:self.lo + self.n] = add_up(g_x, nx, self.lo, self.n)
+                loop(1, nx, lambda d: self.x(d, lax.rem(mx + d, nx)).wait_recv())
+            g_y[my, self.lo:self.lo + self.n] = add_up(g_x, nx, self.lo, self.n).astype(GRAD_DT)
             if ny > 1:
                 far_first(ny, lambda d: self.y(d, my).start())
 
         def send_all(self):
             if ny > 1:
-                loop(1, ny, lambda d: self.y(d, (my + d) % ny).wait_recv())
+                loop(1, ny, lambda d: self.y(d, lax.rem(my + d, ny)).wait_recv())
             g_tot[self.lo:self.lo + self.n] = (add_up(g_y, ny, self.lo, self.n) * norm).astype(GRAD_DT)
             far_first(TILES, lambda d: self.ag(d, me).start())
             g_all[self.piece(me)] = g_tot[self.lo:self.lo + self.n]
@@ -526,22 +533,22 @@
     part_q.send_x()
     gather(3)
     attend_back(1, gmrg)
-    part_q.send_y()
     loop(QB, 2 * QB, backward)
     part_k.scatter()
+    part_q.send_y()
     loop(2 * QB, NB, backward)
     part_v.scatter()
     send_back(back_k, QB)
     send_back(back_v, 2 * QB)
     part_k.send_x()
     part_q.send_all()
-    finish_back(back_q, 0)
     part_v.send_x()
     part_k.send_y()
+    finish_back(back_q, 0)
+    part_v.send_y()
     finish_back(back_k, QB)
-    part_v.send_y()
+    part_k.send_all()
     finish_back(back_v, 2 * QB)
-    part_k.send_all()
     part_v.send_all()
 
     for copy in halo_q + halo_k + halo_v + back_q + back_k + back_v:
@@ -581,6 +588,7 @@
     vmem = pl.BlockSpec(memory_space=pltpu.VMEM)
     scratch = [
         vm((NB, POS, LANES), BF16), vm((8, POS, LANES), BF16),
+        vm((NB, POS, LANES), BF16), vm((NB, POS, LANES), BF16), vm((NB, LANES, LANES), BF16), vm((NB, LANES, LANES), BF16),
         vm((NB, 25, LANES), F32), vm((NB, HD, LANES), F32),
         vm((NB, 12 * PITCH, LANES), F32), vm((NB, 12 * PITCH, LANES), F32),
         vm((NB, POS, LANES), F32), vm((NB, POS, LANES), F32), vm((NB, POS, LANES), F32), vm((NB, POS, LANES), F32),
@@ -592,7 +600,7 @@
         vm((2, 4, NB, 64, LANES), BF16), vm((2, 2, NB, 16, LANES), BF16), vm((2, 2, 48, LANES), BF16),
         vm((32, LANES), F32),
         vm((48, 16, LANES), GRAD_DT), vm((TILES, 3, 16, LANES), GRAD_DT),
-        vm((nx, 3, 16, LANES), F32), vm((ny, 3, 16, LANES), F32),
+        vm((nx, 3, 16, LANES), F32), vm((ny, 3, 16, LANES), GRAD_DT),
         vm((3, 16, LANES), GRAD_DT), vm((48, 16, LANES), GRAD_DT),
         dma((3 * NB + 8,)), dma((2,)),
         dma((4, TILES)), dma((4, TILES)), dma((4, TILES)), dma((4, TILES)),

time: 80.7 us -> 79.7 us (0.988)
  Pallas kernels: 79.9 us -> 78.8 us
    pallas_call x1, Pallas kernels: 78.3 us -> 77.2 us  [local(): pl.pallas_call(functools.partial(kernel, nx, ny, norm), out_shape=(jax.Sh...]
where the time goes in v4:
time: 79.7 us; the launch traced here: 79.5 us
  Pallas kernels  78.8 us (99%)
    pallas_call x1, Pallas kernels, local(): pl.pallas_call(functools.partial(kernel, nx, ny, norm), out_shape=(jax.Sh...  77.2 us
    pallas_call x1, Pallas kernels, local(): pl.pallas_call(write, out_shape=(jax.ShapeDtypeStruct((POS, channels), BF...  1.63 us

profile of v4, /device:TPU:1, one launch (start us, length us, event | category | flops | bytes accessed | tf_op | source)
XLA Modules:
  0.0 79.5 jit_solution(6027597377406206254)
XLA Ops:
  0.6 77.2 %linear_attention.1 = (bf16[256,1536]{1,0:T(8,128)(2,1)S(1)}, bf16[48,16,128]{2,1,0:T(8,128)(2,1)S(1)}) custom-call(bf16[256,1536]{1,0:T(8,128)(2,1)} %bitcast.3, bf16[256,1024]{1,0:T(8,128)(2,1)} %bitcast.4, f32[25,1536]{1,0:T(8,128)} %dw.1, f32[32,1536]{1,0:T(8,128)} %pw.1, s32[1,8]{1,0:T(1,128)} %im_h_in.1, s32[1,8]{1,0:T(1,128)} %im_w_in.1), custom_call_target="tpu_custom_call" | custom-call | tf_op jit(solution)/shard_map/linear_attention/pallas_call | solution.py:611
  77.8 1.6 %write_outputs.1 = (bf16[256,1536]{1,0:T(8,128)(2,1)}, f32[25,1536]{1,0:T(8,128)}, f32[32,1536]{1,0:T(8,128)}) custom-call(bf16[256,1536]{1,0:T(8,128)(2,1)S(1)} %get-tuple-element.8.grad, bf16[48,16,128]{2,1,0:T(8,128)(2,1)S(1)} %get-tuple-element.9.sums), custom_call_target="tpu_custom_call" | custom-call | tf_op jit(solution)/shard_map/write_outputs/pallas_call | solution.py:626

commit v5 on v4

--- a/solution.py
+++ b/solution.py
@@ -283,7 +283,8 @@
             _, rect, keys = relu_terms(scale, 4 + j)
             _, values = terms(scale, 8 + j)
             post_state(scale, j, compact(mm(keys, values, TN)), jnp.sum(rect, axis=0, keepdims=True))
-        loop(0, 4, body)
+        for j in range(4):
+            body(j)
 
     def attend(scale, grads):
         def body(j):
@@ -300,7 +301,8 @@
             grads[j] = jnp.where(raw > 0, grad_query, 0.0)
             post_state(2 + scale, j, compact(mm(queries, grad_parts, TN)),
                        jnp.sum(rect * grad_den, axis=0, keepdims=True))
-        loop(0, 4, body)
+        for j in range(4):
+            body(j)
 
     def attend_back(scale, grads):
         def body(j):
@@ -310,7 +312,8 @@
             grad_key = mm(values, state, NT) + key_sum
             grads[4 + j] = jnp.where(raw > 0, grad_key, 0.0)
             grads[8 + j] = mm(keys, state, NN)
-        loop(0, 4, body)
+        for j in range(4):
+            body(j)
 
     loop(0, NB, lambda c: stage(c, pad, 0))
     stage_corners(pad, 0, 0, NB)
@@ -538,14 +541,14 @@
     part_q.send_y()
     loop(2 * QB, NB, backward)
     part_v.scatter()
+    finish_back(back_q, 0)
     send_back(back_k, QB)
     send_back(back_v, 2 * QB)
     part_k.send_x()
-    part_q.send_all()
     part_v.send_x()
     part_k.send_y()
-    finish_back(back_q, 0)
     part_v.send_y()
+    part_q.send_all()
     finish_back(back_k, QB)
     part_k.send_all()
     finish_back(back_v, 2 * QB)

time: 79.7 us -> 77.9 us (0.977)
  Pallas kernels: 78.8 us -> 77.1 us
    pallas_call x1, Pallas kernels: 77.2 us -> 75.5 us  [local(): pl.pallas_call(functools.partial(kernel, nx, ny, norm), out_shape=(jax.Sh...]
where the time goes in v5:
time: 77.9 us; the launch traced here: 77.7 us
  Pallas kernels  77.1 us (99%)
    pallas_call x1, Pallas kernels, local(): pl.pallas_call(functools.partial(kernel, nx, ny, norm), out_shape=(jax.Sh...  75.5 us
    pallas_call x1, Pallas kernels, local(): pl.pallas_call(write, out_shape=(jax.ShapeDtypeStruct((POS, channels), BF...  1.63 us

profile of v5, /device:TPU:1, one launch (start us, length us, event | category | flops | bytes accessed | tf_op | source)
XLA Modules:
  0.0 77.7 jit_solution(10906360160246190006)
XLA Ops:
  0.6 75.5 %linear_attention.1 = (bf16[256,1536]{1,0:T(8,128)(2,1)S(1)}, bf16[48,16,128]{2,1,0:T(8,128)(2,1)S(1)}) custom-call(bf16[256,1536]{1,0:T(8,128)(2,1)} %bitcast.3, bf16[256,1024]{1,0:T(8,128)(2,1)} %bitcast.4, f32[25,1536]{1,0:T(8,128)} %dw.1, f32[32,1536]{1,0:T(8,128)} %pw.1, s32[1,8]{1,0:T(1,128)} %im_h_in.1, s32[1,8]{1,0:T(1,128)} %im_w_in.1), custom_call_target="tpu_custom_call" | custom-call | tf_op jit(solution)/shard_map/linear_attention/pallas_call | solution.py:614
  76.1 1.6 %write_outputs.1 = (bf16[256,1536]{1,0:T(8,128)(2,1)}, f32[25,1536]{1,0:T(8,128)}, f32[32,1536]{1,0:T(8,128)}) custom-call(bf16[256,1536]{1,0:T(8,128)(2,1)S(1)} %get-tuple-element.8.grad, bf16[48,16,128]{2,1,0:T(8,128)(2,1)S(1)} %get-tuple-element.9.sums), custom_call_target="tpu_custom_call" | custom-call | tf_op jit(solution)/shard_map/write_outputs/pallas_call | solution.py:629
